TPU v7x, 32 devices: a whole 2x2x4 slice. The times are simulated.
32 devices in a mesh: dp: 4 (over y, core), bucket: 8 (over z, x).
Axes of the slice: x: 2, y: 2, z: 4, core: 2. Of those that a mesh axis runs over, the one named last changes fastest.
Arguments:
- frames: bfloat16 [49152, 512], P(('dp', 'bucket')), may hold values from -60 to 60, as said below
- lengths: int32 [4, 256], P('dp'), may hold values from 1 to 48, as said below
- owners: int32 [4, 256], P('dp'), may hold values from 0 to 7, as said below
- upstream: bfloat16 [24576, 512], P(('dp', 'bucket')), may hold values from -6 to 6
- ln_gain: float32 [512], replicated, may hold values from 0.1 to 1.9
- w_in: bfloat16 [512, 1024], replicated, may hold values from -0.25 to 0.25
- w_dw: float32 [512, 31], replicated, may hold values from -1 to 1
- bn_gain: float32 [512], replicated, may hold values from 0.1 to 1.9
- bn_bias: float32 [512], replicated, may hold values from -3 to 3
- w_out: bfloat16 [512, 512], replicated, may hold values from -0.25 to 0.25
Outputs:
- out_frames: bfloat16 [24576, 512], P(('dp', 'bucket'))
- grad_frames: bfloat16 [49152, 512], P(('dp', 'bucket'))
- grad_w_in: float32 [512, 1024], P('bucket')
- grad_w_out: float32 [512, 512], P('bucket')
- grad_w_dw: float32 [512, 31], P('bucket')
- grad_ln_gain: float32 [512], P('bucket')
- grad_bn_gain: float32 [512], replicated
- grad_bn_bias: float32 [512], replicated
Inputs may be any that keep to these rules, and one draw needn't show every extreme that they name: `frames`: frame rows past an utterance's length are not read. In each group every owner receives exactly 4 utterances from each loader shard, their lengths sum to exactly 768 with one of exactly 48, and the lengths an owner receives do not fall with the loader index. `owners`: in each group and loader shard every owner index appears exactly 4 times.
All inputs are finite; a program needn't handle non-finite values.
Results may differ from a plain program's by a relative error of at most 0.013.
Values may be sent and summed in bfloat16 or wider, within the bound.
A program may use at most 128 MiB of HBM per device.

v0:
```python
import jax
import jax.numpy as jnp
from jax import lax
from jax.sharding import PartitionSpec as P

EPSILON = 1e-05


def normalize_rows(frame_rows, ln_gain):
    values = frame_rows.astype(jnp.float32)
    centred = values - jnp.mean(values, axis=1, keepdims=True)
    inverse = lax.rsqrt(jnp.mean(centred * centred, axis=1, keepdims=True) + EPSILON)
    normed = centred * inverse
    return ((normed * ln_gain).astype(jnp.bfloat16), normed, inverse)


def normalize_back(grad_h, normed, inverse, ln_gain):
    scaled = grad_h * ln_gain
    inner_sum = jnp.mean(scaled * normed, axis=1, keepdims=True)
    return inverse * (scaled - jnp.mean(scaled, axis=1, keepdims=True) - normed * inner_sum)


def conv_forward(gated_rows, segment, w_dw):
    width_half = w_dw.shape[1] // 2
    length_all = gated_rows.shape[1]
    padded = jnp.pad(gated_rows, ((0, 0), (width_half, width_half), (0, 0)))
    seg_pad = jnp.pad(segment, ((0, 0), (width_half, width_half)), constant_values=-1)
    result = jnp.zeros(gated_rows.shape, jnp.float32)
    for offset in range(w_dw.shape[1]):
        same_seg = (seg_pad[:, offset : offset + length_all] == segment)[:, :, None]
        shifted = padded[:, offset : offset + length_all].astype(jnp.float32)
        result = result + jnp.where(same_seg, shifted, 0.0) * w_dw[:, offset]
    return result


def conv_backward(grad_conv, gated_rows, segment, w_dw):
    width_half = w_dw.shape[1] // 2
    length_all = gated_rows.shape[1]
    padded = jnp.pad(gated_rows, ((0, 0), (width_half, width_half), (0, 0)))
    grad_pad = jnp.pad(grad_conv, ((0, 0), (width_half, width_half), (0, 0)))
    seg_pad = jnp.pad(segment, ((0, 0), (width_half, width_half)), constant_values=-1)
    grad_gated = jnp.zeros(grad_conv.shape, jnp.float32)
    grad_cols = []
    for offset in range(w_dw.shape[1]):
        same_fwd = (seg_pad[:, offset : offset + length_all] == segment)[:, :, None]
        shifted = jnp.where(
            same_fwd, padded[:, offset : offset + length_all].astype(jnp.float32), 0.0
        )
        grad_cols.append(jnp.sum(shifted * grad_conv, axis=(0, 1)))
        back_start = 2 * width_half - offset
        same_back = (seg_pad[:, back_start : back_start + length_all] == segment)[:, :, None]
        grad_gated = (
            grad_gated
            + jnp.where(same_back, grad_pad[:, back_start : back_start + length_all], 0.0)
            * w_dw[:, offset]
        )
    return (grad_gated, jnp.stack(grad_cols, axis=1))


def local(frames, lengths, owners, upstream, ln_gain, w_in, w_dw, bn_gain, bn_bias, w_out):
    loaders = lax.axis_size("bucket")
    own_index = lax.axis_index("bucket")
    feature_count = frames.shape[1]
    slot_count = lengths.shape[1] // loaders
    span_max = frames.shape[0] // slot_count
    pair_count = slot_count // loaders
    own_rows = upstream.shape[0]
    total_frames = float(own_rows * loaders * lax.axis_size("dp"))
    lens_all = lengths[0].reshape(loaders, slot_count)
    dest_all = owners[0].reshape(loaders, slot_count)
    owner_ids = jnp.arange(loaders, dtype=jnp.int32)
    onehot = (dest_all[:, :, None] == owner_ids[None, None, :]).astype(jnp.int32)
    earlier = jnp.cumsum(onehot, axis=1) - onehot
    ranking = jnp.sum(earlier * onehot, axis=2)
    send_pos = dest_all * pair_count + ranking
    my_pos = lax.dynamic_index_in_dim(send_pos, own_index, 0, keepdims=False)
    send_order = (
        jnp.zeros((slot_count,), jnp.int32).at[my_pos].set(jnp.arange(slot_count, dtype=jnp.int32))
    )
    slot_frames = frames.reshape(slot_count, span_max, feature_count)
    outgoing = jnp.take(slot_frames, send_order, axis=0).reshape(
        loaders, pair_count, span_max, feature_count
    )
    incoming = lax.all_to_all(outgoing, "bucket", split_axis=0, concat_axis=0, tiled=True)
    incoming_rows = incoming.reshape(slot_count * span_max, feature_count)
    pair_ids = jnp.arange(pair_count, dtype=jnp.int32)
    to_me = (dest_all == own_index)[:, :, None] & (ranking[:, :, None] == pair_ids[None, None, :])
    recv_lens = jnp.sum(jnp.where(to_me, lens_all[:, :, None], 0), axis=1).reshape(-1)
    starts = jnp.cumsum(recv_lens) - recv_lens
    position = jnp.arange(span_max, dtype=jnp.int32)
    slot_valid = position[None, :] < recv_lens[:, None]
    row_ids = jnp.arange(own_rows, dtype=jnp.int32)
    row_slot = jnp.sum((starts[None, :] <= row_ids[:, None]).astype(jnp.int32), axis=1) - 1
    row_offset = row_ids - jnp.take(starts, row_slot)
    packed_source = row_slot * span_max + row_offset
    slot_target = jnp.minimum(
        jnp.where(slot_valid, starts[:, None] + position[None, :], own_rows - 1), own_rows - 1
    ).reshape(-1)
    slot_valid_flat = slot_valid.reshape(-1)
    segment = jnp.broadcast_to(
        jnp.arange(slot_count, dtype=jnp.int32)[:, None], (slot_count, span_max)
    )
    work_grad = jnp.where(slot_valid_flat[:, None], jnp.take(upstream, slot_target, axis=0), 0)
    group_count = segment.shape[0]
    group_length = segment.shape[1]
    normed_h, normed, inverse = normalize_rows(incoming_rows, ln_gain)
    projected = jnp.dot(normed_h, w_in, preferred_element_type=jnp.float32)
    linear = projected[:, :feature_count]
    gate_sig = jax.nn.sigmoid(projected[:, feature_count:])
    gated_rows = jnp.where(slot_valid_flat[:, None], linear * gate_sig, 0.0).astype(jnp.bfloat16)
    gated_blocks = gated_rows.reshape(group_count, group_length, feature_count)
    conv_rows = conv_forward(gated_blocks, segment, w_dw).reshape(-1, feature_count)
    masked = jnp.where(slot_valid_flat[:, None], conv_rows, 0.0)
    first_sum, second_sum = lax.psum(
        (jnp.sum(masked, axis=0), jnp.sum(masked * masked, axis=0)), ("dp", "bucket")
    )
    centre = first_sum / total_frames
    variance = second_sum / total_frames - centre * centre
    bn_inverse = lax.rsqrt(variance + EPSILON)
    bn_normed = (conv_rows - centre) * bn_inverse
    bn_value = bn_normed * bn_gain + bn_bias
    bn_sig = jax.nn.sigmoid(bn_value)
    swished = (bn_value * bn_sig).astype(jnp.bfloat16)
    out_rows = jnp.dot(swished, w_out, preferred_element_type=jnp.float32).astype(jnp.bfloat16)
    out_frames = jnp.take(out_rows, packed_source, axis=0)
    grad_wout = jnp.einsum("rd,re->de", swished, work_grad, preferred_element_type=jnp.float32)
    grad_swish = jnp.einsum("re,de->rd", work_grad, w_out, preferred_element_type=jnp.float32)
    grad_bn_rows = grad_swish * (bn_sig * (1.0 + bn_value * (1.0 - bn_sig)))
    bias_total, gain_total = lax.psum(
        (jnp.sum(grad_bn_rows, axis=0), jnp.sum(grad_bn_rows * bn_normed, axis=0)), ("dp", "bucket")
    )
    grad_conv = jnp.where(
        slot_valid_flat[:, None],
        bn_gain
        * bn_inverse
        * (grad_bn_rows - bias_total / total_frames - bn_normed * (gain_total / total_frames)),
        0.0,
    )
    grad_gated, grad_wdw = conv_backward(
        grad_conv.reshape(group_count, group_length, feature_count), gated_blocks, segment, w_dw
    )
    grad_gated = jnp.where(slot_valid_flat[:, None], grad_gated.reshape(-1, feature_count), 0.0)
    grad_proj = jnp.concatenate(
        [grad_gated * gate_sig, grad_gated * linear * gate_sig * (1.0 - gate_sig)], axis=1
    ).astype(jnp.bfloat16)
    grad_win = jnp.einsum("rd,rf->df", normed_h, grad_proj, preferred_element_type=jnp.float32)
    grad_h = jnp.einsum("rf,df->rd", grad_proj, w_in, preferred_element_type=jnp.float32)
    grad_ln = jnp.sum(grad_h * normed, axis=0)
    grad_work = jnp.where(
        slot_valid_flat[:, None], normalize_back(grad_h, normed, inverse, ln_gain), 0.0
    ).astype(jnp.bfloat16)
    returned = lax.all_to_all(
        grad_work.reshape(loaders, pair_count, span_max, feature_count),
        "bucket",
        split_axis=0,
        concat_axis=0,
        tiled=True,
    )
    grad_frames = jnp.take(
        returned.reshape(slot_count, span_max, feature_count), my_pos, axis=0
    ).reshape(-1, feature_count)
    row_sums = (
        lax.psum_scatter(grad_win, "bucket", scatter_dimension=0, tiled=True),
        lax.psum_scatter(grad_wout, "bucket", scatter_dimension=0, tiled=True),
        lax.psum_scatter(grad_wdw, "bucket", scatter_dimension=0, tiled=True),
        lax.psum_scatter(grad_ln, "bucket", scatter_dimension=0, tiled=True),
    )
    shares = (
        lax.psum(row_sums[0].astype(jnp.bfloat16), "dp").astype(jnp.float32),
        lax.psum(row_sums[1].astype(jnp.bfloat16), "dp").astype(jnp.float32),
        lax.psum(row_sums[2].astype(jnp.bfloat16), "dp").astype(jnp.float32),
        lax.psum(row_sums[3].astype(jnp.bfloat16), "dp").astype(jnp.float32),
    )
    return (
        out_frames,
        grad_frames,
        shares[0],
        shares[1],
        shares[2],
        shares[3],
        gain_total,
        bias_total,
    )


def solution(mesh):
    placed = (
        P(("dp", "bucket"), None),
        P("dp", None),
        P("dp", None),
        P(("dp", "bucket"), None),
        P(),
        P(),
        P(),
        P(),
        P(),
        P(),
    )
    return jax.shard_map(
        local,
        mesh=mesh,
        in_specs=placed,
        out_specs=(
            P(("dp", "bucket"), None),
            P(("dp", "bucket"), None),
            P("bucket", None),
            P("bucket", None),
            P("bucket", None),
            P("bucket"),
            P(),
            P(),
        ),
        check_vma=False,
    )
```

profile of v0, /device:TPU:1, one launch (start us, length us, event | category | flops | bytes accessed | tf_op | source)
XLA Modules:
  0.0 466.7 jit_solution(478238532868027686)
XLA Ops:
  12.6 2.8 broadcast_select_fusion.1
  15.4 6.3 %all-to-all-start = ((bf16[8,4,48,512]{3,2,1,0:T(8,128)(2,1)}), bf16[8,4,48,512]{3,2,1,0:T(8,128)(2,1)}, u32[]{:S(2)}, u32[]{:S(2)}) async-start(bf16[8,4,48,512]{3,2,1,0:T(8,128)(2,1)} %bitcast.243), calls=%async_computation | async-start | bytes 3145728 | tf_op jit(solution)/shard_map/all_to_all | solution.py:84
  23.6 5.4 %gather_fusion.1 = bf16[1536,512]{1,0:T(8,128)(2,1)} fusion(bf16[768,512]{1,0:T(8,128)(2,1)S(1)} %copy-done.1, s32[2048]{0:T(1024)S(1)} %pad_clamp_fusion), kind=kCustom, calls=%fused_computation.3 | custom fusion | bytes 3151872 | tf_op jit(solution)/shard_map/jit(_take)/gather | solution.py:103
  29.1 28.9 %all-to-all-done = bf16[8,4,48,512]{3,2,1,0:T(8,128)(2,1)} async-done(((bf16[8,4,48,512]{3,2,1,0:T(8,128)(2,1)}), bf16[8,4,48,512]{3,2,1,0:T(8,128)(2,1)}, u32[]{:S(2)}, u32[]{:S(2)}) %all-to-all-start) | async-done | bytes 1572896 | tf_op jit(solution)/shard_map/all_to_all | solution.py:84
  59.8 2.1 multiply_reduce_fusion.35
  68.8 20.7 %select_reduce_fusion = (f32[512]{0:T(512)S(1)}, f32[512]{0:T(512)S(1)}, f32[32,48,512]{2,1,0:T(8,128)}) fusion(pred[32,48]{1,0:T(8,128)(4,1)S(1)} %iota_compare_fusion.3, f32[512]{0:T(512)S(1)} %bitcast.355, pred[32,48]{1,0:T(8,128)(4,1)S(1)} %bitcast.323, f32[512]{0:T(512)S(1)} %bitcast.357, pred[32,48]{1,0:T(8,128)(4,1)S(1)} %bitcast.320, ...), kind=kLoop, calls=%fused_computation.243 | loop fusion | flops 99089408 | bytes 4833792 | tf_op jit(solution)/shard_map/reduce_sum | solution.py:115
  89.5 38.2 %all-reduce.4 = (f32[512]{0:T(512)S(1)}, f32[512]{0:T(512)S(1)}) all-reduce(f32[512]{0:T(512)S(1)} %get-tuple-element.42, f32[512]{0:T(512)S(1)} %get-tuple-element.41), channel_id=1, replica_groups=mesh['dp'=4,'bucket'=8] {'dp','bucket'}, use_global_device_ids=true, to_apply=%region_11.13 | all-reduce | flops 1024 | bytes 8192 | tf_op jit(solution)/shard_map/psum | solution.py:114
  127.7 4.2 multiply_convert_fusion.2
  131.9 4.3 fusion.111
  136.2 41.4 %all-reduce.3 = (f32[512]{0:T(512)S(1)}, f32[512]{0:T(512)S(1)}) all-reduce(f32[512]{0:T(512)S(1)} %get-tuple-element.45, f32[512]{0:T(512)S(1)} %get-tuple-element.44), channel_id=1, replica_groups=mesh['dp'=4,'bucket'=8] {'dp','bucket'}, use_global_device_ids=true, to_apply=%region_15.17 | all-reduce | flops 1024 | bytes 8192 | tf_op jit(solution)/shard_map/psum | solution.py:129
  178.1 5.5 %multiply_reduce_fusion.16 = (f32[512]{0:T(512)S(1)}, f32[1536,512]{1,0:T(8,128)S(1)}) fusion(f32[1536,512]{1,0:T(8,128)} %copy-done.4, f32[512]{0:T(512)S(1)} %get-tuple-element.164, f32[1536,512]{1,0:T(8,128)} %get-tuple-element.162, f32[512]{0:T(512)S(1)} %get-tuple-element.165, f32[512]{0:T(512)S(1)} %get-tuple-element.83, pred[1536]{0:T(1024)(128)(4,1)S(1)} %lt.126, ...), kind=kLoop, calls=%fused_computation.182 | loop fusion | flops 11009536 | bytes 15738368 | tf_op jit(solution)/shard_map/reduce_sum | solution.py:49
  185.6 7.1 %multiply_reduce_fusion.10 = (f32[512]{0:T(512)S(1)}, f32[512]{0:T(512)S(1)}, f32[512]{0:T(512)S(1)}, f32[512]{0:T(512)S(1)}, f32[512]{0:T(512)S(1)}, /*index=5*...) fusion(f32[32,48,512]{2,1,0:T(8,128)S(1)} %bitcast.234, pred[32,48]{1,0:T(8,128)(4,1)S(1)} %bitcast.297, ...), kind=kLoop, calls=%fused_computation.176 | loop fusion | flops 28306944 | bytes 4750848 | tf_op jit(solution)/shard_map/reduce_sum | solution.py:49
  192.7 6.7 %multiply_reduce_fusion.20 = (f32[512]{0:T(512)S(1)}, f32[512]{0:T(512)S(1)}, f32[512]{0:T(512)S(1)}, f32[512]{0:T(512)S(1)}, f32[512]{0:T(512)S(1)}, /*index=5*...) fusion(f32[32,48,512]{2,1,0:T(8,128)S(1)} %bitcast.235, pred[32,48]{1,0:T(8,128)(4,1)S(1)} %bitcast.270, ...), kind=kLoop, calls=%fused_computation.186 | loop fusion | flops 28306944 | bytes 4750848 | tf_op jit(solution)/shard_map/reduce_sum | solution.py:49
  199.4 6.5 %multiply_reduce_fusion.1 = (f32[512]{0:T(512)S(1)}, f32[512]{0:T(512)S(1)}, f32[512]{0:T(512)S(1)}, f32[512]{0:T(512)S(1)}, f32[512]{0:T(512)S(1)}, /*index=5*/...) fusion(f32[32,48,512]{2,1,0:T(8,128)S(1)} %bitcast.236, pred[32,48]{1,0:T(8,128)(4,1)S(1)} %bitcast.324, ...), kind=kLoop, calls=%fused_computation.167 | loop fusion | flops 28306944 | bytes 4750848 | tf_op jit(solution)/shard_map/reduce_sum | solution.py:49
  207.0 4.0 fusion.110
  211.3 49.1 %fusion.73 = f32[32,48,512]{2,1,0:T(8,128)} fusion(f32[32,48,512]{2,1,0:T(8,128)} %bitcast.237, f32[512]{0:T(512)S(1)} %bitcast.356, f32[512]{0:T(512)S(1)} %bitcast.358, f32[512]{0:T(512)S(1)} %bitcast.362, f32[512]{0:T(512)S(1)} %bitcast.364, f32[512]{0:T(512)S(1)} %bitcast.366, f32[512]{0:T(512)S(1)} %bitcast.368, f32[512]{0:T(512)S(1)} %bitcast.370, ...), kind=kLoop, calls=%fused_computation.139 | loop fusion | flops 71565312 | bytes 6401024 | tf_op jit(solution)/shard_map/add | solution.py:53
  260.4 4.7 %multiply_convert_fusion.1 = (bf16[1536,512]{1,0:T(8,128)(2,1)S(1)}, bf16[1536,512]{1,0:T(8,128)(2,1)S(1)}) fusion(f32[32,48,512]{2,1,0:T(8,128)} %fusion.73, pred[1536]{0:T(1024)(128)(4,1)S(1)} %lt.126, f32[1536,1024]{1,0:T(8,128)} %copy-done.3), kind=kLoop, calls=%fused_computation.201 | loop fusion | flops 8650752 | bytes 12584448 | tf_op jit(solution)/shard_map/convert.1
  266.3 3.2 fusion.95
  269.5 4.8 %multiply_reduce_fusion = (f32[512]{0:T(512)S(1)}, f32[1536]{0:T(1024)S(1)}, f32[1536]{0:T(1024)S(1)}, f32[1536,512]{1,0:T(8,128)S(1)}) fusion(bf16[8,4,48,512]{3,2,1,0:T(8,128)(2,1)} %all-to-all-done, f32[1536]{0:T(1024)S(1)} %rsqrt.15, f32[1536]{0:T(1024)S(1)} %div.33, f32[512]{0:T(512)S(1)} %copy-done.41, bf16[512,1024]{1,0:T(8,128)(2,1)} %param.17, ...), kind=kOutput, calls=%fused_computation.166 | convolution fusion | flops 1623978496 | bytes 8941568 | tf_op jit(solution)/shard_map/rf,df->rd/dot_general | solution.py:147
  274.3 3.4 select_convert_fusion
  277.8 4.4 all-to-all-start.1
  284.3 4.5 fusion.102
  289.8 16.2 %compare_and_fusion.1 = (pred[768]{0:T(1024)(128)(4,1)S(1)}, s32[768]{0:T(1024)S(1)}) fusion(s32[768]{0:T(1024)S(1)} %convert_reduce_fusion.1, pred[768]{0:T(1024)(128)(4,1)S(1)} %get-tuple-element.70, pred[768]{0:T(1024)(128)(4,1)S(1)} %get-tuple-element.68, pred[768]{0:T(1024)(128)(4,1)S(1)} %get-tuple-element.69, ...), kind=kLoop, calls=%fused_computation.315 | loop fusion | flops 32256 | bytes 29284 | tf_op jit(solution)/shard_map/jit(_take)/and | solution.py:125
  306.1 2.5 convolution_convert_fusion
  308.6 3.3 gather_fusion
  311.9 18.1 %all-reduce.2 = bf16[512]{0:T(512)(128)(2,1)S(1)} all-reduce(f32[512]{0:T(512)S(1)} %get-tuple-element.9), channel_id=5, replica_groups=mesh['dp'=4,'bucket'=8] {'bucket'}, use_global_device_ids=true, to_apply=%region_56.58.clone | all-reduce | flops 512 | bytes 3072
  330.1 2.2 broadcast_select_fusion.2
  333.1 11.2 %all-reduce.5 = (bf16[64,31]{0,1:T(8,128)(2,1)S(1)}, bf16[64]{0:T(256)(128)(2,1)S(1)}) all-reduce(bf16[64,31]{0,1:T(8,128)(2,1)S(1)} %copy.42, bf16[64]{0:T(256)(128)(2,1)S(1)} %dynamic-slice.3), channel_id=1, replica_groups=mesh['dp'=4,'bucket'=8] {'dp'}, use_global_device_ids=true, to_apply=%region_54.56 | all-reduce | flops 2048 | bytes 8192 | tf_op jit(solution)/shard_map/psum | solution.py:171
  345.5 5.9 %reduce-scatter.8.cloned.1.call-done = f32[64,512]{1,0:T(8,128)} async-done(((f32[512,512]{1,0:T(8,128)}), f32[64,512]{1,0:T(8,128)}) %reduce-scatter.8.cloned.1.call-update) | async-done | bytes 131088 | tf_op jit(solution)/shard_map/reduce_scatter | solution.py:164
  353.0 2.1 gather_fusion.3
  355.0 67.9 %reduce-scatter.6.cloned.1.call-done = f32[64,1024]{1,0:T(8,128)} async-done(((f32[512,1024]{1,0:T(8,128)}), f32[64,1024]{1,0:T(8,128)}) %reduce-scatter.6.cloned.1.call-update) | async-done | bytes 262160 | tf_op jit(solution)/shard_map/reduce_scatter | solution.py:163
  425.9 31.1 %all-reduce.9.cloned.1.call-done = (bf16[64,1024]{1,0:T(8,128)(2,1)}, bf16[64,512]{1,0:T(8,128)(2,1)}) async-done(((bf16[64,1024]{1,0:T(8,128)(2,1)}, bf16[64,512]{1,0:T(8,128)(2,1)}), (bf16[64,1024]{1,0:T(8,128)(2,1)}, bf16[64,512]{1,0:T(8,128)(2,1)})) %all-reduce.9.cloned.1.call-update) | async-done | bytes 196624 | tf_op jit(solution)/shard_map/psum | solution.py:169
  (178 shorter events, 32.5 us)
Async XLA Ops:
  7.2 3.6 copy-start
  12.6 9.2 %copy-start.46 = (s32[1,256]{1,0:T(1,128)S(1)}, s32[1,256]{1,0:T(1,128)}, u32[]{:S(2)}) copy-start(s32[1,256]{1,0:T(1,128)} %param.13) | copy-start | bytes 3076
  12.6 11.0 %copy-start.1 = (bf16[768,512]{1,0:T(8,128)(2,1)S(1)}, bf16[768,512]{1,0:T(8,128)(2,1)}, u32[]{:S(2)}) copy-start(bf16[768,512]{1,0:T(8,128)(2,1)} %param.15) | copy-start | bytes 2359300
  15.4 42.6 %all-to-all-start = ((bf16[8,4,48,512]{3,2,1,0:T(8,128)(2,1)}), bf16[8,4,48,512]{3,2,1,0:T(8,128)(2,1)}, u32[]{:S(2)}, u32[]{:S(2)}) async-start(bf16[8,4,48,512]{3,2,1,0:T(8,128)(2,1)} %bitcast.243), calls=%async_computation | async-start | bytes 3145728 | tf_op jit(solution)/shard_map/all_to_all | solution.py:84
  21.7 310.5 %reduce-scatter.10.cloned.1.call-start = ((), (), s32[]{:S(2)}) async-start(), calls=%async_computation.7 | async-start | bytes 294912
  23.6 5.4 %copy-start.9 = (f32[512,31]{0,1:T(8,128)S(1)}, f32[512,31]{0,1:T(8,128)}, u32[]{:S(2)}) copy-start(f32[512,31]{0,1:T(8,128)} %param.18) | copy-start | bytes 190468
  29.0 33.0 %copy-start.41 = (f32[512]{0:T(512)S(1)}, f32[512]{0:T(512)}, u32[]{:S(2)}) copy-start(f32[512]{0:T(512)} %param.16) | copy-start | bytes 6148
  29.0 102.9 %copy-start.45 = (pred[1536]{0:T(1024)(128)(4,1)}, pred[1536]{0:T(1024)(128)(4,1)S(1)}, u32[]{:S(2)}) copy-start(pred[1536]{0:T(1024)(128)(4,1)S(1)} %compare_and_fusion) | copy-start | bytes 4612
  29.1 34.9 %copy-start.47 = (bf16[512,1024]{1,0:T(8,128)(2,1)S(1)}, bf16[512,1024]{1,0:T(8,128)(2,1)}, u32[]{:S(2)}) copy-start(bf16[512,1024]{1,0:T(8,128)(2,1)} %param.17) | copy-start | bytes 3145732
  65.9 2.7 copy-start.3
  65.9 2.7 copy-start.10
  65.9 2.6 copy-start.11
  65.9 2.6 copy-start.12
  65.9 2.6 copy-start.13
  65.9 2.6 copy-start.14
  65.9 2.6 copy-start.15
  66.0 2.6 copy-start.16
  66.0 2.6 copy-start.17
  66.0 2.6 copy-start.18
  68.5 59.2 %copy-start.40 = (f32[512]{0:T(512)S(1)}, f32[512]{0:T(512)}, u32[]{:S(2)}) copy-start(f32[512]{0:T(512)} %param.19) | copy-start | bytes 6148
  68.5 59.2 %copy-start.42 = (f32[512]{0:T(512)S(1)}, f32[512]{0:T(512)}, u32[]{:S(2)}) copy-start(f32[512]{0:T(512)} %param.20) | copy-start | bytes 6148
  127.7 4.2 copy-start.5
  127.7 4.2 copy-start.48
  131.9 4.3 copy-start.4
  177.5 6.1 %copy-start.44 = (f32[512]{0:T(512)}, f32[512]{0:T(512)S(1)}, u32[]{:S(2)}) copy-start(f32[512]{0:T(512)S(1)} %get-tuple-element.72) | copy-start | bytes 6148
  183.7 15.7 %copy-start.2 = (f32[1536,512]{1,0:T(8,128)}, f32[1536,512]{1,0:T(8,128)S(1)}, u32[]{:S(2)}) copy-start(f32[1536,512]{1,0:T(8,128)S(1)} %get-tuple-element.80) | copy-start | bytes 9437188
  206.9 144.5 %reduce-scatter.8.cloned.1.call-start = ((), (), s32[]{:S(2)}) async-start(), calls=%async_computation.6 | async-start | bytes 1179648 | tf_op jit(solution)/shard_map/reduce_scatter | solution.py:164
  211.1 211.8 %reduce-scatter.6.cloned.1.call-start = ((), (), s32[]{:S(2)}) async-start(), calls=%async_computation.5 | async-start | bytes 2359296 | tf_op jit(solution)/shard_map/reduce_scatter | solution.py:163
  260.4 5.9 %copy-start.7 = (bf16[1536,512]{1,0:T(8,128)(2,1)S(1)}, bf16[1536,512]{1,0:T(8,128)(2,1)}, u32[]{:S(2)}) copy-start(bf16[1536,512]{1,0:T(8,128)(2,1)} %copy-done.6) | copy-start | bytes 4718596
  277.8 4.5 copy-start.49
  277.8 75.2 %all-to-all-start.1 = ((bf16[8,4,48,512]{3,2,1,0:T(8,128)(2,1)}), bf16[8,4,48,512]{3,2,1,0:T(8,128)(2,1)}, u32[]{:S(2)}, u32[]{:S(2)}) async-start(bf16[8,4,48,512]{3,2,1,0:T(8,128)(2,1)} %bitcast.73), calls=%async_computation.1 | async-start | bytes 3145728 | tf_op jit(solution)/shard_map/all_to_all | solution.py:152
  282.2 174.8 %all-reduce.9.cloned.1.call-start = ((), (), s32[]{:S(2)}) async-start(), calls=%async_computation.8 | async-start | bytes 393216 | tf_op jit(solution)/shard_map/psum | solution.py:169
  (24 other events, 58.0 us)
Sparse Core Ops, SparseCore 0:
  207.1 60.8 reduce-scatter.9
  271.3 80.0 reduce-scatter.7
  355.0 67.8 reduce-scatter.5
  425.8 31.1 all-reduce.8
where the time goes:
time: 470 us; the launch traced here: 467 us
  other arithmetic  155 us (33%)
  waiting for transfers between devices  134 us (29%)
  blocking collectives  109 us (23%)
  local copies, waits for them, and re-layouts  21.6 us (5%)
  matrix products  20.6 us (4%)
  between operations  15.4 us (3%)
  starting transfers between devices  11.2 us (2%)
    reduce_scatter x1, waiting for transfers between devices, local(): lax.psum_scatter(grad_win, 'bucket', scatter_dimension=0, tiled=True)  67.9 us
    add x1, other arithmetic, conv_backward(): grad_gated + jnp.where(same_back, grad_pad[:, back_start:back_start + len...  49.1 us
    psum x1, blocking collectives, local(): lax.psum((jnp.sum(grad_bn_rows, axis=0), jnp.sum(grad_bn_rows * bn_normed...  41.4 us
    psum x1, blocking collectives, local(): lax.psum((jnp.sum(masked, axis=0), jnp.sum(masked * masked, axis=0)), ('d...  38.2 us
    psum x1, waiting for transfers between devices, local(): lax.psum(row_sums[0].astype(jnp.bfloat16), 'dp').astype(jnp.float32)  31.1 us
    all_to_all x1, waiting for transfers between devices, local(): lax.all_to_all(outgoing, 'bucket', split_axis=0, concat_axis=0, tiled=True)  28.9 us
    reduce_sum x5, other arithmetic, conv_backward(): grad_cols.append(jnp.sum(shifted * grad_conv, axis=(0, 1)))  27.7 us
    reduce_sum x1, other arithmetic, local(): jnp.sum(masked, axis=0)  20.7 us
  transfers between devices with their start and end apart: 6, of which 4 were waited for; matrix products, arithmetic and copies ran while one was open for 25% of the time, Pallas kernels for 0%

commit v1 on v0

v1 whole, which is shorter than its diff:
```python
import functools

import jax
import jax.numpy as jnp
from jax import lax
from jax.experimental import pallas as pl
from jax.experimental.pallas import tpu as pltpu
from jax.sharding import PartitionSpec as P

EPSILON = 1e-05
LANES = 128
SUB = 8
MESH = pl.DeviceIdType.MESH
VMEM_LIMIT = 48 << 20


def lane(c):
    return slice(c * LANES, (c + 1) * LANES)


def row_of(packed, first, blocks):
    return jnp.concatenate([packed[first + c : first + c + 1] for c in range(blocks)], axis=1)


def live_rows(lens_ref, first, count, span, width):
    position = lax.broadcasted_iota(jnp.int32, (span, width), 0)
    return [position < lens_ref[first + i] for i in range(count)]


def keep_live(values, masks, span):
    parts = [
        jnp.where(masks[i], values[i * span : (i + 1) * span], 0.0) for i in range(len(masks))
    ]
    return jnp.concatenate(parts, axis=0)


def layer_norm(frame_rows):
    values = frame_rows.astype(jnp.float32)
    centred = values - jnp.mean(values, axis=1, keepdims=True)
    inverse = lax.rsqrt(jnp.mean(centred * centred, axis=1, keepdims=True) + EPSILON)
    return centred * inverse, inverse


def project(frame_rows, gain, w_in):
    normed, inverse = layer_norm(frame_rows)
    h = (normed * gain).astype(jnp.bfloat16)
    projected = jnp.dot(h, w_in, preferred_element_type=jnp.float32)
    half = projected.shape[1] // 2
    return normed, inverse, h, projected[:, :half], jax.nn.sigmoid(projected[:, half:])


def shifted_sum(padded, weight, span, taps):
    total = None
    for residue in range(SUB):
        part = None
        for k in range(residue, taps + 1, SUB):
            if k == 0:
                continue
            term = padded[k - residue : k - residue + span + SUB] * weight(k)
            part = term if part is None else part + term
        if residue:
            part = pltpu.roll(part, span + SUB - residue, 0)
        part = part[:span]
        total = part if total is None else total + part
    return total


def forward_kernel(group, span, taps, lens_ref, frames_ref, gain_ref, w_in_ref, w_dw_ref,
                   conv_ref, sums_ref, padded):
    step = pl.program_id(0)
    blocks = conv_ref.shape[1] // LANES
    edge = (padded.shape[2] - span) // 2

    @pl.when(step == 0)
    def _():
        padded[...] = jnp.zeros_like(padded)
        sums_ref[...] = jnp.zeros_like(sums_ref)

    masks = live_rows(lens_ref, step * group, group, span, conv_ref.shape[1])
    _, _, _, linear, gate = project(frames_ref[...], gain_ref[...], w_in_ref[...])
    gated = keep_live(linear * gate, masks, span).astype(jnp.bfloat16).astype(jnp.float32)
    for u in range(group):
        for c in range(blocks):
            padded[u, c, edge : edge + span] = gated[u * span : (u + 1) * span, lane(c)]

    def one(u, carry):
        live = lax.broadcasted_iota(jnp.int32, (span, LANES), 0) < lens_ref[step * group + u]
        start = pl.multiple_of(u * span, SUB)
        for c in range(blocks):
            conv = shifted_sum(
                padded[u, c], lambda k: w_dw_ref[k - 1 : k, lane(c)], span, taps
            )
            conv_ref[pl.ds(start, span), lane(c)] = conv
            masked = jnp.where(live, conv, 0.0)
            sums_ref[c : c + 1] += jnp.sum(masked, axis=0, keepdims=True)
            sums_ref[blocks + c : blocks + c + 1] += jnp.sum(
                masked * masked, axis=0, keepdims=True
            )
        return carry

    lax.fori_loop(0, group, one, 0)


def batch_norm(total_ref, conv, total_frames, blocks):
    packed = total_ref[...]
    centre = row_of(packed, 0, blocks) / total_frames
    variance = row_of(packed, blocks, blocks) / total_frames - centre * centre
    inverse = lax.rsqrt(variance + EPSILON)
    return (conv - centre) * inverse, inverse


def middle_kernel(group, span, total_frames, lens_ref, conv_ref, dy_ref, total_ref, bn_gain_ref,
                  bn_bias_ref, w_out_ref, out_ref, grad_bn_ref, sums_ref, grad_wout_ref):
    step = pl.program_id(0)
    width = conv_ref.shape[1]
    blocks = width // LANES

    @pl.when(step == 0)
    def _():
        sums_ref[...] = jnp.zeros_like(sums_ref)
        grad_wout_ref[...] = jnp.zeros_like(grad_wout_ref)

    masks = live_rows(lens_ref, step * group, group, span, width)
    dy = keep_live(dy_ref[...].astype(jnp.float32), masks, span).astype(jnp.bfloat16)
    w_out = w_out_ref[...]
    bn_normed, _ = batch_norm(total_ref, conv_ref[...], total_frames, blocks)
    bn = bn_normed * bn_gain_ref[...] + bn_bias_ref[...]
    sig = jax.nn.sigmoid(bn)
    swished = (bn * sig).astype(jnp.bfloat16)
    out_ref[...] = jnp.dot(swished, w_out, preferred_element_type=jnp.float32).astype(jnp.bfloat16)
    grad_wout_ref[...] += lax.dot_general(
        swished, dy, (((0,), (0,)), ((), ())), preferred_element_type=jnp.float32
    )
    grad_swish = lax.dot_general(
        dy, w_out, (((1,), (1,)), ((), ())), preferred_element_type=jnp.float32
    )
    grad_bn = grad_swish * (sig * (1.0 + bn * (1.0 - sig)))
    grad_bn_ref[...] = grad_bn
    bias_row = jnp.sum(grad_bn, axis=0, keepdims=True)
    gain_row = jnp.sum(grad_bn * bn_normed, axis=0, keepdims=True)
    for c in range(blocks):
        sums_ref[c : c + 1] += bias_row[:, lane(c)]
        sums_ref[blocks + c : blocks + c + 1] += gain_row[:, lane(c)]


def backward_kernel(group, span, taps, total_frames, lens_ref, frames_ref, conv_ref, grad_bn_ref,
                    total_ref, back_ref, gain_ref, bn_gain_ref, w_in_ref, w_dw_ref, wout_ref,
                    grad_frames_ref, packed_ref, padded, grad_pad, gated_grad, w_acc, win_acc,
                    ln_acc, flat):
    step = pl.program_id(0)
    width = conv_ref.shape[1]
    blocks = width // LANES
    edge = (padded.shape[2] - span) // 2

    @pl.when(step == 0)
    def _():
        padded[...] = jnp.zeros_like(padded)
        grad_pad[...] = jnp.zeros_like(grad_pad)
        w_acc[...] = jnp.zeros_like(w_acc)
        win_acc[...] = jnp.zeros_like(win_acc)
        ln_acc[...] = jnp.zeros_like(ln_acc)

    masks = live_rows(lens_ref, step * group, group, span, width)
    w_in = w_in_ref[...]
    normed, inverse, h, linear, gate = project(frames_ref[...], gain_ref[...], w_in)
    gated = keep_live(linear * gate, masks, span).astype(jnp.bfloat16).astype(jnp.float32)
    bn_normed, bn_inverse = batch_norm(total_ref, conv_ref[...], total_frames, blocks)
    back = back_ref[...]
    bias_mean = row_of(back, 0, blocks) / total_frames
    gain_mean = row_of(back, blocks, blocks) / total_frames
    grad_conv = keep_live(
        bn_gain_ref[...] * bn_inverse * (grad_bn_ref[...] - bias_mean - bn_normed * gain_mean),
        masks,
        span,
    )
    for u in range(group):
        for c in range(blocks):
            rows = slice(u * span, (u + 1) * span)
            padded[u, c, edge : edge + span] = gated[rows, lane(c)]
            grad_pad[u, c, edge : edge + span] = grad_conv[rows, lane(c)]

    def one(u, carry):
        start = pl.multiple_of(u * span, SUB)
        for c in range(blocks):
            grads = grad_pad[u, c]
            gated_grad[pl.ds(start, span), lane(c)] = shifted_sum(
                grads, lambda k: w_dw_ref[taps - k : taps - k + 1, lane(c)], span, taps
            )
            inner = grads[edge - SUB : edge + span + SUB]
            frame = padded[u, c]
            for residue in range(SUB):
                moved = inner if residue == 0 else pltpu.roll(inner, residue, 0)
                moved = moved[SUB:]
                for k in range(residue, taps + 1, SUB):
                    if k == 0:
                        continue
                    term = moved * frame[k - residue : k - residue + span + SUB]
                    part = term[:SUB]
                    for i in range(1, span // SUB + 1):
                        part = part + term[i * SUB : (i + 1) * SUB]
                    w_acc[c, k - 1] += part
        return carry

    lax.fori_loop(0, group, one, 0)

    grad_gated = keep_live(gated_grad[...], masks, span)
    left = grad_gated * gate
    grad_a = jnp.concatenate(
        [left.astype(jnp.bfloat16), (left * linear * (1.0 - gate)).astype(jnp.bfloat16)], axis=1
    )
    win_acc[...] += lax.dot_general(
        h, grad_a, (((0,), (0,)), ((), ())), preferred_element_type=jnp.float32
    )
    grad_h = lax.dot_general(
        grad_a, w_in, (((1,), (1,)), ((), ())), preferred_element_type=jnp.float32
    )
    ln_acc[...] += jnp.sum(grad_h * normed, axis=0, keepdims=True)
    scaled = grad_h * gain_ref[...]
    inner_mean = jnp.mean(scaled * normed, axis=1, keepdims=True)
    grad_x = inverse * (scaled - jnp.mean(scaled, axis=1, keepdims=True) - normed * inner_mean)
    grad_frames_ref[...] = keep_live(grad_x, masks, span).astype(jnp.bfloat16)

    @pl.when(step == pl.num_programs(0) - 1)
    def _():
        owners = packed_ref.shape[0]
        share = width // owners
        wide = w_in.shape[1] // LANES
        for c in range(blocks):
            flat[...] = jnp.zeros_like(flat)
            for k in range(taps):
                flat[k : k + 1] = jnp.sum(w_acc[c, k], axis=0, keepdims=True)
            flat[taps : taps + 1] = ln_acc[:, lane(c)]
            turned = flat[...].T.astype(jnp.bfloat16)
            for i in range(LANES // share):
                packed_ref[c * (LANES // share) + i, (wide + blocks) * share :] = turned[
                    i * share : (i + 1) * share
                ]
        for j in range(owners):
            rows = slice(j * share, (j + 1) * share)
            for c in range(wide):
                packed_ref[j, c * share : (c + 1) * share] = win_acc[rows, lane(c)].astype(
                    jnp.bfloat16
                )
            for c in range(blocks):
                packed_ref[j, (wide + c) * share : (wide + c + 1) * share] = wout_ref[
                    rows, lane(c)
                ].astype(jnp.bfloat16)


def whole(shape):
    return pl.BlockSpec(shape, lambda i, *_: (0,) * len(shape))


def sum_kernel(groups, owners, part_ref, out_ref, slots, send_sems, recv_sems):
    count = groups * owners
    me = lax.axis_index("dp") * owners + lax.axis_index("bucket")
    barrier = pltpu.get_barrier_semaphore()

    def peer_of(i):
        other = lax.rem(me + i, count)
        return (other // owners, lax.rem(other, owners))

    def greet(i, carry):
        pl.semaphore_signal(barrier, inc=1, device_id=peer_of(i), device_id_type=MESH)
        return carry

    lax.fori_loop(1, count, greet, 0)
    pl.semaphore_wait(barrier, count - 1)

    def copy_to(i):
        return pltpu.make_async_remote_copy(
            src_ref=part_ref,
            dst_ref=slots.at[me],
            send_sem=send_sems.at[i],
            recv_sem=recv_sems.at[me],
            device_id=peer_of(i),
            device_id_type=MESH,
        )

    def send(i, carry):
        copy_to(i).start()
        return carry

    lax.fori_loop(1, count, send, 0)
    slots[me] = part_ref[...]

    def receive(i, carry):
        source = lax.rem(me + i, count)
        pltpu.make_async_remote_copy(
            src_ref=part_ref,
            dst_ref=slots.at[source],
            send_sem=send_sems.at[i],
            recv_sem=recv_sems.at[source],
            device_id=peer_of(i),
            device_id_type=MESH,
        ).wait_recv()
        return carry

    lax.fori_loop(1, count, receive, 0)
    out_ref[...] = lax.fori_loop(
        1, count, lambda i, total: total + slots[i], slots[0]
    )

    def sent(i, carry):
        copy_to(i).wait_send()
        return carry

    lax.fori_loop(1, count, sent, 0)


def sum_everywhere(part, collective_id):
    groups, owners = lax.axis_size("dp"), lax.axis_size("bucket")
    count = groups * owners
    return pl.pallas_call(
        functools.partial(sum_kernel, groups, owners),
        out_shape=jax.ShapeDtypeStruct(part.shape, part.dtype),
        in_specs=[pl.BlockSpec(memory_space=pltpu.VMEM)],
        out_specs=pl.BlockSpec(memory_space=pltpu.VMEM),
        scratch_shapes=[
            pltpu.VMEM((count,) + part.shape, part.dtype),
            pltpu.SemaphoreType.DMA((count,)),
            pltpu.SemaphoreType.DMA((count,)),
        ],
        compiler_params=pltpu.CompilerParams(collective_id=collective_id, has_side_effects=True),
        cost_estimate=pl.CostEstimate(flops=10**6, bytes_accessed=2 * 10**7, transcendentals=0),
        name="sum_everywhere_%d" % collective_id,
    )(part)


def reduce_kernel(groups, owners, src, out, first, first_sum, second, second_sum, third, mine,
                  core_sems, pair_sems, row_sems, all_sems):
    dp, me = lax.axis_index("dp"), lax.axis_index("bucket")
    halves = groups // 2
    core, side = lax.rem(dp, 2), dp // 2
    chunk = core * halves + side
    partner = side * 2 + (1 - core)
    barrier = pltpu.get_barrier_semaphore()

    def group_peer(i):
        return lax.rem(dp + i, groups)

    def owner_peer(i):
        return lax.rem(me + i, owners)

    def greet_group(i, carry):
        pl.semaphore_signal(barrier, inc=1, device_id=(group_peer(i), me), device_id_type=MESH)
        return carry

    def greet_owner(i, carry):
        pl.semaphore_signal(barrier, inc=1, device_id=(dp, owner_peer(i)), device_id_type=MESH)
        return carry

    lax.fori_loop(1, groups, greet_group, 0)
    lax.fori_loop(1, owners, greet_owner, 0)
    pl.semaphore_wait(barrier, groups + owners - 2)

    def remote(source, target, sems, i, j, device):
        return pltpu.make_async_remote_copy(
            src_ref=source,
            dst_ref=target,
            send_sem=sems.at[0, i],
            recv_sem=sems.at[1, j],
            device_id=device,
            device_id_type=MESH,
        )

    swap = remote(src.at[1 - core], first, core_sems, 0, 0, (partner, me))
    swap.start()
    swap.wait()

    def add_first(j, carry):
        total = src[core, j].astype(jnp.float32) + first[j].astype(jnp.float32)
        first_sum[j] = total.astype(jnp.bfloat16)
        return carry

    lax.fori_loop(0, halves * owners, add_first, 0)

    def to_side(i, arriving):
        other = lax.rem(side + i, halves)
        slot = other if arriving else side
        return remote(
            first_sum.at[pl.ds(other * owners, owners)],
            second.at[slot],
            pair_sems, i, slot,
            (other * 2 + core, me),
        )

    for i in range(1, halves):
        to_side(i, False).start()
    for i in range(1, halves):
        to_side(i, True).wait_recv()

    def add_second(j, carry):
        total = first_sum[side * owners + j].astype(jnp.float32)
        for i in range(1, halves):
            total = total + second[lax.rem(side + i, halves), j].astype(jnp.float32)
        second_sum[j] = total.astype(jnp.bfloat16)
        return carry

    lax.fori_loop(0, owners, add_second, 0)

    def to_owner(i, arriving):
        other = owner_peer(i)
        slot = other if arriving else me
        return remote(second_sum.at[other], third.at[slot], row_sems, i, slot, (dp, other))

    def send_owner(i, carry):
        to_owner(i, False).start()
        return carry

    def wait_owner(i, carry):
        to_owner(i, True).wait_recv()
        return carry

    lax.fori_loop(1, owners, send_owner, 0)
    lax.fori_loop(1, owners, wait_owner, 0)
    third[me] = second_sum[me]
    total = lax.fori_loop(
        1, owners, lambda i, t: t + third[i].astype(jnp.float32), third[0].astype(jnp.float32)
    )
    mine[...] = total.astype(jnp.bfloat16)

    def to_group(i, arriving):
        other = group_peer(i)
        device = other if arriving else dp
        slot = lax.rem(device, 2) * halves + device // 2
        return remote(mine, out.at[slot], all_sems, i, slot, (other, me))

    def send_group(i, carry):
        to_group(i, False).start()
        return carry

    def wait_group(i, carry):
        to_group(i, True).wait_recv()
        return carry

    lax.fori_loop(1, groups, send_group, 0)
    out[chunk] = mine[...]
    lax.fori_loop(1, groups, wait_group, 0)

    def sent_owner(i, carry):
        to_owner(i, False).wait_send()
        return carry

    def sent_group(i, carry):
        to_group(i, False).wait_send()
        return carry

    for i in range(1, halves):
        to_side(i, False).wait_send()
    lax.fori_loop(1, owners, sent_owner, 0)
    lax.fori_loop(1, groups, sent_group, 0)


def reduce_rows(packed, collective_id):
    groups, owners = lax.axis_size("dp"), lax.axis_size("bucket")
    halves = groups // 2
    rows = packed.shape[1] // groups
    source = packed.reshape(owners, 2, halves, rows, LANES).transpose(1, 2, 0, 3, 4)
    source = source.reshape(2, halves * owners, rows, LANES)
    kind = jnp.bfloat16
    return pl.pallas_call(
        functools.partial(reduce_kernel, groups, owners),
        out_shape=jax.ShapeDtypeStruct((groups, rows, LANES), kind),
        in_specs=[pl.BlockSpec(memory_space=pltpu.VMEM)],
        out_specs=pl.BlockSpec(memory_space=pltpu.VMEM),
        scratch_shapes=[
            pltpu.VMEM((halves * owners, rows, LANES), kind),
            pltpu.VMEM((halves * owners, rows, LANES), kind),
            pltpu.VMEM((halves, owners, rows, LANES), kind),
            pltpu.VMEM((owners, rows, LANES), kind),
            pltpu.VMEM((owners, rows, LANES), kind),
            pltpu.VMEM((rows, LANES), kind),
            pltpu.SemaphoreType.DMA((2, 1)),
            pltpu.SemaphoreType.DMA((2, halves)),
            pltpu.SemaphoreType.DMA((2, owners)),
            pltpu.SemaphoreType.DMA((2, groups)),
        ],
        compiler_params=pltpu.CompilerParams(collective_id=collective_id, has_side_effects=True),
        cost_estimate=pl.CostEstimate(flops=10**7, bytes_accessed=6 * 10**7, transcendentals=0),
        name="reduce_rows",
    )(source)


def pick(array, index):
    return array.at[index].get(mode="promise_in_bounds")


def local(frames, lengths, owners, upstream, ln_gain, w_in, w_dw, bn_gain, bn_bias, w_out):
    loaders = lax.axis_size("bucket")
    own_index = lax.axis_index("bucket")
    width = frames.shape[1]
    taps = w_dw.shape[1]
    slot_count = lengths.shape[1] // loaders
    span = frames.shape[0] // slot_count
    pair_count = slot_count // loaders
    own_rows = upstream.shape[0]
    blocks = width // LANES
    total_frames = float(own_rows * loaders * lax.axis_size("dp"))
    lens_all = lengths[0].reshape(loaders, slot_count)
    dest_all = owners[0].reshape(loaders, slot_count)
    owner_ids = jnp.arange(loaders, dtype=jnp.int32)
    onehot = (dest_all[:, :, None] == owner_ids[None, None, :]).astype(jnp.int32)
    earlier = jnp.cumsum(onehot, axis=1) - onehot
    ranking = jnp.sum(earlier * onehot, axis=2)
    send_pos = dest_all * pair_count + ranking
    my_pos = lax.dynamic_index_in_dim(send_pos, own_index, 0, keepdims=False)
    my_lens = lax.dynamic_index_in_dim(lens_all, own_index, 0, keepdims=False)
    slot_ids = jnp.arange(slot_count, dtype=jnp.int32)
    send_order = jnp.sum(
        jnp.where(my_pos[None, :] == slot_ids[:, None], slot_ids[None, :], 0), axis=1
    )
    pair_ids = jnp.arange(pair_count, dtype=jnp.int32)
    to_me = (dest_all == own_index)[:, :, None] & (ranking[:, :, None] == pair_ids[None, None, :])
    recv_lens = jnp.sum(jnp.where(to_me, lens_all[:, :, None], 0), axis=1).reshape(-1)
    starts = jnp.cumsum(recv_lens) - recv_lens
    position = jnp.arange(span, dtype=jnp.int32)
    row_ids = jnp.arange(own_rows, dtype=jnp.int32)
    reached = (starts[None, :] <= row_ids[:, None]).astype(jnp.int32)
    row_slot = jnp.sum(reached, axis=1) - 1
    row_start = jnp.max(reached * starts[None, :], axis=1)
    packed_source = row_slot * span + row_ids - row_start
    slot_target = jnp.minimum(starts[:, None] + position[None, :], own_rows - 1).reshape(-1)

    outgoing = pick(upstream, slot_target).reshape(loaders, pair_count, span, width)
    incoming = lax.all_to_all(outgoing, "bucket", split_axis=0, concat_axis=0, tiled=True)

    group = 4
    steps = slot_count // group
    rows = group * span
    edge = (taps + 1) // 2
    row_block = pl.BlockSpec((rows, width), lambda i, *_: (i, 0))
    all_rows = slot_count * span
    gain_row, bn_gain_row, bn_bias_row = ln_gain[None], bn_gain[None], bn_bias[None]
    w_taps = jnp.pad(w_dw.T, ((0, 1), (0, 0)))
    sums_shape = (2 * blocks, LANES)
    params = pltpu.CompilerParams(
        dimension_semantics=("arbitrary",), vmem_limit_bytes=VMEM_LIMIT
    )
    padded_shape = pltpu.VMEM((group, blocks, span + 2 * edge, LANES), jnp.float32)

    conv, part = pl.pallas_call(
        functools.partial(forward_kernel, group, span, taps),
        grid_spec=pltpu.PrefetchScalarGridSpec(
            num_scalar_prefetch=1,
            grid=(steps,),
            in_specs=[row_block, whole((1, width)), whole(w_in.shape), whole(w_taps.shape)],
            out_specs=[row_block, whole(sums_shape)],
            scratch_shapes=[padded_shape],
        ),
        out_shape=[
            jax.ShapeDtypeStruct((all_rows, width), jnp.float32),
            jax.ShapeDtypeStruct(sums_shape, jnp.float32),
        ],
        compiler_params=params,
        cost_estimate=pl.CostEstimate(
            flops=2 * 10**9, bytes_accessed=4 * 10**7, transcendentals=0
        ),
        name="forward",
    )(my_lens, frames, gain_row, w_in, w_taps)
    totals = sum_everywhere(part, 0)

    work_grad = pick(incoming.reshape(slot_count, span, width), my_pos).reshape(all_rows, width)
    out_rows, grad_bn, back_part, grad_wout = pl.pallas_call(
        functools.partial(middle_kernel, group, span, total_frames),
        grid_spec=pltpu.PrefetchScalarGridSpec(
            num_scalar_prefetch=1,
            grid=(steps,),
            in_specs=[
                row_block, row_block, whole(sums_shape), whole((1, width)), whole((1, width)),
                whole(w_out.shape),
            ],
            out_specs=[row_block, row_block, whole(sums_shape), whole(w_out.shape)],
        ),
        out_shape=[
            jax.ShapeDtypeStruct((all_rows, width), jnp.bfloat16),
            jax.ShapeDtypeStruct((all_rows, width), jnp.float32),
            jax.ShapeDtypeStruct(sums_shape, jnp.float32),
            jax.ShapeDtypeStruct(w_out.shape, jnp.float32),
        ],
        compiler_params=params,
        cost_estimate=pl.CostEstimate(
            flops=3 * 10**9, bytes_accessed=2 * 10**7, transcendentals=0
        ),
        name="middle",
    )(my_lens, conv, work_grad, totals, bn_gain_row, bn_bias_row, w_out)

    leaving = pick(out_rows.reshape(slot_count, span, width), send_order).reshape(
        loaders, pair_count, span, width
    )
    arrived = lax.all_to_all(leaving, "bucket", split_axis=0, concat_axis=0, tiled=True)
    back_totals = sum_everywhere(back_part, 1)

    share = width // loaders
    packed_rows = (w_in.shape[1] // LANES + blocks + 1) * share
    grad_frames, packed = pl.pallas_call(
        functools.partial(backward_kernel, group, span, taps, total_frames),
        grid_spec=pltpu.PrefetchScalarGridSpec(
            num_scalar_prefetch=1,
            grid=(steps,),
            in_specs=[
                row_block, row_block, row_block, whole(sums_shape), whole(sums_shape),
                whole((1, width)), whole((1, width)), whole(w_in.shape), whole(w_taps.shape),
                whole(w_out.shape),
            ],
            out_specs=[row_block, whole((loaders, packed_rows, LANES))],
            scratch_shapes=[
                padded_shape,
                padded_shape,
                pltpu.VMEM((rows, width), jnp.float32),
                pltpu.VMEM((blocks, taps + 1, SUB, LANES), jnp.float32),
                pltpu.VMEM(w_in.shape, jnp.float32),
                pltpu.VMEM((1, width), jnp.float32),
                pltpu.VMEM((LANES, LANES), jnp.float32),
            ],
        ),
        out_shape=[
            jax.ShapeDtypeStruct((all_rows, width), jnp.bfloat16),
            jax.ShapeDtypeStruct((loaders, packed_rows, LANES), jnp.bfloat16),
        ],
        compiler_params=params,
        cost_estimate=pl.CostEstimate(
            flops=6 * 10**9, bytes_accessed=8 * 10**7, transcendentals=0
        ),
        name="backward",
    )(
        my_lens, frames, conv, grad_bn, totals, back_totals, gain_row, bn_gain_row, w_in, w_taps,
        grad_wout,
    )
    reduced = reduce_rows(packed, 2).reshape(-1, share, LANES).astype(jnp.float32)
    out_frames = pick(arrived.reshape(slot_count * span, width), packed_source)
    wide = w_in.shape[1] // LANES
    grad_win = reduced[:wide].transpose(1, 0, 2).reshape(share, -1)
    grad_wo = reduced[wide : wide + blocks].transpose(1, 0, 2).reshape(share, -1)
    last = reduced[wide + blocks]
    flat_back = back_totals.reshape(2, width)
    return (
        out_frames,
        grad_frames,
        grad_win,
        grad_wo,
        last[:, :taps],
        last[:, taps],
        flat_back[1],
        flat_back[0],
    )


def solution(mesh):
    placed = (
        P(("dp", "bucket"), None),
        P("dp", None),
        P("dp", None),
        P(("dp", "bucket"), None),
        P(),
        P(),
        P(),
        P(),
        P(),
        P(),
    )
    return jax.shard_map(
        local,
        mesh=mesh,
        in_specs=placed,
        out_specs=(
            P(("dp", "bucket"), None),
            P(("dp", "bucket"), None),
            P("bucket", None),
            P("bucket", None),
            P("bucket", None),
            P("bucket"),
            P(),
            P(),
        ),
        check_vma=False,
    )
```

time: 470 us -> 207 us (0.44)
  Pallas kernels: 0 us -> 158 us
  other arithmetic: 155 us -> 5.11 us
  waiting for transfers between devices: 134 us -> 0.01 us
  blocking collectives: 109 us -> 0 us
  matrix products: 20.6 us -> 0 us
  between operations: 15.4 us -> 0.98 us
  local copies, waits for them, and re-layouts: 21.6 us -> 30.5 us
    pallas_call x0 -> x6, Pallas kernels: none -> 158 us  [the longest x2 67.6 us: sum_everywhere(): pl.pallas_call(functools.partial(sum_kernel, groups, owners), out_shape=j...]
    psum x3 -> x0, blocking collectives: 90.7 us -> none  [the longest x1 41.4 us: local(): lax.psum((jnp.sum(grad_bn_rows, axis=0), jnp.sum(grad_bn_rows * bn_normed...]
    reduce_scatter x2 -> x0, waiting for transfers between devices: 73.8 us -> none  [the longest x1 67.9 us: local(): lax.psum_scatter(grad_win, 'bucket', scatter_dimension=0, tiled=True)]
    reduce_sum x9 -> x2, other arithmetic: 52.3 us -> 0.21 us  [the longest x1 0.11 us: local(): jnp.sum(jnp.where(my_pos[None, :] == slot_ids[:, None], slot_ids[None, :]...]
    add x2 -> x0, other arithmetic: 49.1 us -> none  [the longest x1 49.1 us: conv_backward(): grad_gated + jnp.where(same_back, grad_pad[:, back_start:back_start + len...]
    psum x1 -> x0, waiting for transfers between devices: 31.1 us -> none  [local(): lax.psum(row_sums[0].astype(jnp.bfloat16), 'dp').astype(jnp.float32)]
    all_to_all x1, waiting for transfers between devices: 28.9 us -> 0.01 us  [local(): lax.all_to_all(outgoing, 'bucket', split_axis=0, concat_axis=0, tiled=True)]
    dot_general x6 -> x0, matrix products: 20.6 us -> none  [the longest x1 4.83 us: local(): jnp.einsum('rf,df->rd', grad_proj, w_in, preferred_element_type=jnp.float32)]
  transfers between devices with their start and end apart: 6 -> 2, of which waited for: 4 -> 0; matrix products, arithmetic and copies ran while one was open for 25% -> 3% of each run, Pallas kernels for 0% -> 73%
where the time goes in v1:
time: 207 us; the launch traced here: 206 us
  Pallas kernels  158 us (76%)
  local copies, waits for them, and re-layouts  30.5 us (15%)
  starting transfers between devices  11 us (5%)
  other arithmetic  5.11 us (2%)
    pallas_call x2, Pallas kernels, sum_everywhere(): pl.pallas_call(functools.partial(sum_kernel, groups, owners), out_shape=j...  67.6 us
    pallas_call x1, Pallas kernels, local(): pl.pallas_call(functools.partial(backward_kernel, group, span, taps, tota...  34.6 us
    pallas_call x1, Pallas kernels, reduce_rows(): pl.pallas_call(functools.partial(reduce_kernel, groups, owners), out_shap...  31.4 us
    gather x4, local copies, waits for them, and re-layouts, pick(): return array.at[index].get(mode='promise_in_bounds')  15.7 us
    pallas_call x1, Pallas kernels, local(): pl.pallas_call(functools.partial(forward_kernel, group, span, taps), grid...  15.5 us
    unnamed x42, local copies, waits for them, and re-layouts  9.05 us
    pallas_call x1, Pallas kernels, local(): pl.pallas_call(functools.partial(middle_kernel, group, span, total_frames...  8.84 us
    all_to_all x1, starting transfers between devices, local(): lax.all_to_all(outgoing, 'bucket', split_axis=0, concat_axis=0, tiled=True)  6.62 us
  transfers between devices with their start and end apart: 2, of which 0 were waited for; matrix products, arithmetic and copies ran while one was open for 3% of the time, Pallas kernels for 73%

profile of v1, /device:TPU:1, one launch (start us, length us, event | category | flops | bytes accessed | tf_op | source)
XLA Modules:
  0.0 205.5 jit_solution(2210689904338148454)
XLA Ops:
  0.7 0.5 broadcast.145
  1.2 1.3 reduce.11
  2.6 1.3 reduce.12
  4.1 0.7 fusion.9
  6.2 5.4 %gather_fusion = bf16[1536,512]{1,0:T(8,128)(2,1)} fusion(bf16[768,512]{1,0:T(8,128)(2,1)S(1)} %copy-done, s32[2048]{0:T(1024)S(1)} %pad_clamp_fusion), kind=kCustom, calls=%fused_computation | custom fusion | bytes 3151872 | tf_op jit(solution)/shard_map/gather | solution.py:486
  11.6 6.6 %all-to-all-start = ((bf16[8,4,48,512]{3,2,1,0:T(8,128)(2,1)}), bf16[8,4,48,512]{3,2,1,0:T(8,128)(2,1)}, u32[]{:S(2)}, u32[]{:S(2)}) async-start(bf16[8,4,48,512]{3,2,1,0:T(8,128)(2,1)} %bitcast.56), calls=%async_computation | async-start | bytes 3145728 | tf_op jit(solution)/shard_map/all_to_all | solution.py:526
  18.3 15.5 %forward.1 = (f32[1536,512]{1,0:T(8,128)S(1)}, f32[8,128]{1,0:T(8,128)S(1)}) custom-call(s32[32]{0:T(128)S(1)} %get-tuple-element.28.lens_ref, bf16[1536,512]{1,0:T(8,128)(2,1)S(1)} %copy-done.7, f32[1,512]{1,0:T(1,128)S(1)} %bitcast.51, bf16[512,1024]{1,0:T(8,128)(2,1)S(1)} %copy-done.9, f32[32,512]{1,0:T(8,128)S(1)} %pad.4.w_dw_ref), custom_call_target="tpu_custom_call" | custom-call | flops 2000000000 | bytes 40000000 | tf_op jit(solution)/shard_map/forward/pallas_call | solution.py:542
  33.8 0.6 copy-done.6
  34.4 1.7 copy-done.14
  36.1 25.5 %sum_everywhere_0.1.total_ref = f32[8,128]{1,0:T(8,128)} custom-call(f32[8,128]{1,0:T(8,128)} %copy-done.6), custom_call_target="tpu_custom_call" | custom-call | flops 1000000 | bytes 20000000 | tf_op jit(solution)/shard_map/sum_everywhere_0/pallas_call | solution.py:314
  61.8 2.1 %gather_fusion.1 = bf16[32,48,512]{2,1,0:T(8,128)(2,1)S(1)} fusion(bf16[32,48,512]{2,1,0:T(8,128)(2,1)} %bitcast.4, s32[1024]{0:T(1024)S(1)} %pad_clamp_fusion.3), kind=kCustom, calls=%fused_computation.1 | custom fusion | bytes 3145856 | tf_op jit(solution)/shard_map/gather | solution.py:486
  63.9 1.0 copy-done.10
  65.0 8.8 %middle.1 = (bf16[1536,512]{1,0:T(8,128)(2,1)S(1)}, f32[1536,512]{1,0:T(8,128)}, f32[8,128]{1,0:T(8,128)S(1)}, f32[512,512]{1,0:T(8,128)S(1)}) custom-call(s32[32]{0:T(128)S(1)} %get-tuple-element.28.lens_ref, f32[1536,512]{1,0:T(8,128)} %copy-done.14, bf16[1536,512]{1,0:T(8,128)(2,1)S(1)} %bitcast.48, f32[8,128]{1,0:T(8,128)S(1)} %copy-done.4, ...), custom_call_target="tpu_custom_call" | custom-call | flops 3000000000 | bytes 20000000 | tf_op jit(solution)/shard_map/middle/pallas_call | solution.py:564
  73.8 1.1 copy-done.1
  74.9 0.6 copy-done.5
  75.5 1.0 copy-done.15
  76.5 3.3 %gather_fusion.2 = bf16[32,48,512]{2,1,0:T(8,128)(2,1)} fusion(bf16[32,48,512]{2,1,0:T(8,128)(2,1)} %bitcast.49, s32[1024]{0:T(1024)S(1)} %pad_clamp_fusion.2), kind=kCustom, calls=%fused_computation.2 | custom fusion | bytes 3145856 | tf_op jit(solution)/shard_map/gather | solution.py:486
  79.8 4.4 %all-to-all-start.1 = ((bf16[8,4,48,512]{3,2,1,0:T(8,128)(2,1)}), bf16[8,4,48,512]{3,2,1,0:T(8,128)(2,1)}, u32[]{:S(2)}, u32[]{:S(2)}) async-start(bf16[8,4,48,512]{3,2,1,0:T(8,128)(2,1)} %bitcast.57), calls=%async_computation.1 | async-start | bytes 3145728 | tf_op jit(solution)/shard_map/all_to_all | solution.py:591
  84.4 42.1 %sum_everywhere_1.1.back_ref = f32[8,128]{1,0:T(8,128)} custom-call(f32[8,128]{1,0:T(8,128)} %copy-done.5), custom_call_target="tpu_custom_call" | custom-call | flops 1000000 | bytes 20000000 | tf_op jit(solution)/shard_map/sum_everywhere_1/pallas_call | solution.py:314
  126.5 0.7 copy-done.2
  127.2 1.2 copy-done.16
  128.4 34.6 %backward.1 = (bf16[1536,512]{1,0:T(8,128)(2,1)}, bf16[8,832,128]{2,1,0:T(8,128)(2,1)S(1)}) custom-call(s32[32]{0:T(128)S(1)} %get-tuple-element.28.lens_ref, bf16[1536,512]{1,0:T(8,128)(2,1)S(1)} %copy-done.8, f32[1536,512]{1,0:T(8,128)} %copy-done.14, f32[1536,512]{1,0:T(8,128)} %get-tuple-element.19.grad_bn_ref, f32[8,128]{1,0:T(8,128)S(1)} %copy-done.4, ...), custom_call_target="tpu_custom_call" | custom-call | flops 6000000000 | bytes 80000000 | tf_op jit(solution)/shard_map/backward/pallas_call | solution.py:596
  163.0 1.3 copy.61
  164.3 31.4 %reduce_rows.1 = bf16[4,208,128]{2,1,0:T(8,128)(2,1)} custom-call(bf16[2,16,208,128]{3,2,1,0:T(8,128)(2,1)} %bitcast.55), custom_call_target="tpu_custom_call" | custom-call | flops 10000000 | bytes 60000000 | tf_op jit(solution)/shard_map/reduce_rows/pallas_call | solution.py:462
  195.7 1.0 convert.1
  196.6 0.7 slice.40
  197.4 0.6 slice.41
  198.1 0.5 slice_bitcast_fusion.4
  198.6 0.6 slice_bitcast_fusion.2
  199.2 0.7 copy_bitcast_fusion.1
  199.8 0.7 copy_bitcast_fusion
  200.5 5.0 %gather_fusion.3 = bf16[768,512]{1,0:T(8,128)(2,1)} fusion(bf16[1536,512]{1,0:T(8,128)(2,1)} %bitcast.15, s32[1024]{0:T(1024)S(1)} %pad_clamp_fusion.1), kind=kCustom, calls=%fused_computation.3 | custom fusion | bytes 1575936 | tf_op jit(solution)/shard_map/gather | solution.py:486
  (63 shorter events, 2.0 us)
Async XLA Ops:
  0.6 5.6 %copy-start = (bf16[768,512]{1,0:T(8,128)(2,1)S(1)}, bf16[768,512]{1,0:T(8,128)(2,1)}, u32[]{:S(2)}) copy-start(bf16[768,512]{1,0:T(8,128)(2,1)} %param.13) | copy-start | bytes 2359300
  5.5 0.5 copy-start.18
  11.6 6.6 %copy-start.17 = (f32[512,31]{0,1:T(8,128)S(1)}, f32[512,31]{0,1:T(8,128)}, u32[]{:S(2)}) copy-start(f32[512,31]{0,1:T(8,128)} %param.16) | copy-start | bytes 190468
  11.6 6.7 %copy-start.7 = (bf16[1536,512]{1,0:T(8,128)(2,1)S(1)}, bf16[1536,512]{1,0:T(8,128)(2,1)}, u32[]{:S(2)}) copy-start(bf16[1536,512]{1,0:T(8,128)(2,1)} %frames_ref.3) | copy-start | bytes 4718596
  11.6 6.7 %copy-start.9 = (bf16[512,1024]{1,0:T(8,128)(2,1)S(1)}, bf16[512,1024]{1,0:T(8,128)(2,1)}, u32[]{:S(2)}) copy-start(bf16[512,1024]{1,0:T(8,128)(2,1)} %w_in_ref.3) | copy-start | bytes 3145732
  11.6 6.7 %copy-start.12 = (f32[512]{0:T(512)S(1)}, f32[512]{0:T(512)}, u32[]{:S(2)}) copy-start(f32[512]{0:T(512)} %param.14) | copy-start | bytes 6148
  11.6 50.1 %all-to-all-start = ((bf16[8,4,48,512]{3,2,1,0:T(8,128)(2,1)}), bf16[8,4,48,512]{3,2,1,0:T(8,128)(2,1)}, u32[]{:S(2)}, u32[]{:S(2)}) async-start(bf16[8,4,48,512]{3,2,1,0:T(8,128)(2,1)} %bitcast.56), calls=%async_computation | async-start | bytes 3145728 | tf_op jit(solution)/shard_map/all_to_all | solution.py:526
  33.8 0.6 copy-start.6
  34.4 1.7 copy-start.14
  61.8 2.1 %copy-start.4 = (f32[8,128]{1,0:T(8,128)S(1)}, f32[8,128]{1,0:T(8,128)}, u32[]{:S(2)}) copy-start(f32[8,128]{1,0:T(8,128)} %sum_everywhere_0.1.total_ref) | copy-start | bytes 12292
  61.8 2.1 %copy-start.11 = (f32[512]{0:T(512)S(1)}, f32[512]{0:T(512)}, u32[]{:S(2)}) copy-start(f32[512]{0:T(512)} %param.18) | copy-start | bytes 6148
  61.8 2.1 %copy-start.13 = (f32[512]{0:T(512)S(1)}, f32[512]{0:T(512)}, u32[]{:S(2)}) copy-start(f32[512]{0:T(512)} %param.17) | copy-start | bytes 6148
  63.9 1.0 copy-start.10
  73.8 1.1 copy-start.1
  74.9 0.6 copy-start.5
  75.5 1.0 copy-start.15
  79.8 4.4 %copy-start.19 = (s32[32]{0:T(128)S(1)}, s32[32]{0:T(128)}, u32[]{:S(2)}) copy-start(s32[32]{0:T(128)} %copy-done.18) | copy-start | bytes 388
  79.8 46.7 %copy-start.8 = (bf16[1536,512]{1,0:T(8,128)(2,1)S(1)}, bf16[1536,512]{1,0:T(8,128)(2,1)}, u32[]{:S(2)}) copy-start(bf16[1536,512]{1,0:T(8,128)(2,1)} %frames_ref.3) | copy-start | bytes 4718596
  79.8 120.7 %all-to-all-start.1 = ((bf16[8,4,48,512]{3,2,1,0:T(8,128)(2,1)}), bf16[8,4,48,512]{3,2,1,0:T(8,128)(2,1)}, u32[]{:S(2)}, u32[]{:S(2)}) async-start(bf16[8,4,48,512]{3,2,1,0:T(8,128)(2,1)} %bitcast.57), calls=%async_computation.1 | async-start | bytes 3145728 | tf_op jit(solution)/shard_map/all_to_all | solution.py:591
  126.5 0.7 copy-start.2
  127.2 1.2 copy-start.16
  164.3 34.3 %copy-start.3 = (f32[8,128]{1,0:T(8,128)S(1)}, f32[8,128]{1,0:T(8,128)}, u32[]{:S(2)}) copy-start(f32[8,128]{1,0:T(8,128)} %sum_everywhere_1.1.back_ref) | copy-start | bytes 12292

commit v2 on v1

--- a/solution.py
+++ b/solution.py
@@ -24,7 +24,7 @@
 
 def live_rows(lens_ref, first, count, span, width):
     position = lax.broadcasted_iota(jnp.int32, (span, width), 0)
-    return [position < lens_ref[first + i] for i in range(count)]
+    return [position < lens_ref[0, first + i] for i in range(count)]
 
 
 def keep_live(values, masks, span):
@@ -84,7 +84,7 @@
             padded[u, c, edge : edge + span] = gated[u * span : (u + 1) * span, lane(c)]
 
     def one(u, carry):
-        live = lax.broadcasted_iota(jnp.int32, (span, LANES), 0) < lens_ref[step * group + u]
+        live = lax.broadcasted_iota(jnp.int32, (span, LANES), 0) < lens_ref[0, step * group + u]
         start = pl.multiple_of(u * span, SUB)
         for c in range(blocks):
             conv = shifted_sum(
@@ -121,13 +121,17 @@
         grad_wout_ref[...] = jnp.zeros_like(grad_wout_ref)
 
     masks = live_rows(lens_ref, step * group, group, span, width)
-    dy = keep_live(dy_ref[...].astype(jnp.float32), masks, span).astype(jnp.bfloat16)
+    slots = [lens_ref[1, step * group + i] for i in range(group)]
+    arrived = jnp.concatenate([dy_ref[slot] for slot in slots], axis=0)
+    dy = keep_live(arrived.astype(jnp.float32), masks, span).astype(jnp.bfloat16)
     w_out = w_out_ref[...]
     bn_normed, _ = batch_norm(total_ref, conv_ref[...], total_frames, blocks)
     bn = bn_normed * bn_gain_ref[...] + bn_bias_ref[...]
     sig = jax.nn.sigmoid(bn)
     swished = (bn * sig).astype(jnp.bfloat16)
-    out_ref[...] = jnp.dot(swished, w_out, preferred_element_type=jnp.float32).astype(jnp.bfloat16)
+    out = jnp.dot(swished, w_out, preferred_element_type=jnp.float32).astype(jnp.bfloat16)
+    for i in range(group):
+        out_ref[slots[i]] = out[i * span : (i + 1) * span]
     grad_wout_ref[...] += lax.dot_general(
         swished, dy, (((0,), (0,)), ((), ())), preferred_element_type=jnp.float32
     )
@@ -247,6 +251,69 @@
                 ].astype(jnp.bfloat16)
 
 
+def plan_kernel(slots, lens_ref, owners_ref, up_ref, out_ref, meta_ref, stage, counts):
+    me = lax.axis_index("bucket")
+    own_rows, width = up_ref.shape
+    span = out_ref.shape[1]
+    blocks = width // LANES
+    loaders = lens_ref.shape[1] // slots
+    pairs = slots // loaders
+    for c in range(blocks):
+        stage[c, :own_rows] = up_ref[:, lane(c)].astype(jnp.float32)
+        stage[c, own_rows:] = jnp.zeros((span, LANES), jnp.float32)
+
+    def look(i, carry):
+        found, start = carry
+        mine = owners_ref[0, i] == me
+
+        @pl.when(mine)
+        def _():
+            meta_ref[2, found] = start
+            for c in range(blocks):
+                out_ref[found, :, lane(c)] = stage[c, pl.ds(start, span)].astype(jnp.bfloat16)
+
+        return found + mine.astype(jnp.int32), start + jnp.where(mine, lens_ref[0, i], 0)
+
+    lax.fori_loop(0, loaders * slots, look, (jnp.int32(0), jnp.int32(0)))
+
+    def clear(i, carry):
+        counts[i] = 0
+        return carry
+
+    lax.fori_loop(0, loaders, clear, 0)
+
+    def place(i, carry):
+        owner = owners_ref[0, me * slots + i]
+        rank = counts[owner]
+        counts[owner] = rank + 1
+        meta_ref[0, i] = lens_ref[0, me * slots + i]
+        meta_ref[1, i] = owner * pairs + rank
+        return carry
+
+    lax.fori_loop(0, slots, place, 0)
+
+
+def finish_kernel(meta_ref, arrived_ref, reduced_ref, out_ref, win_ref, wout_ref, last_ref, stage):
+    slots, span, width = arrived_ref.shape
+    own_rows = out_ref.shape[0]
+    blocks = width // LANES
+    wide = win_ref.shape[1] // LANES
+
+    def place(u, carry):
+        start = meta_ref[2, u]
+        for c in range(blocks):
+            stage[c, pl.ds(start, span)] = arrived_ref[u, :, lane(c)].astype(jnp.float32)
+        return carry
+
+    lax.fori_loop(0, slots, place, 0)
+    for c in range(blocks):
+        out_ref[:, lane(c)] = stage[c, :own_rows].astype(jnp.bfloat16)
+        wout_ref[:, lane(c)] = reduced_ref[wide + c].astype(jnp.float32)
+    for c in range(wide):
+        win_ref[:, lane(c)] = reduced_ref[c].astype(jnp.float32)
+    last_ref[...] = reduced_ref[wide + blocks].astype(jnp.float32)
+
+
 def whole(shape):
     return pl.BlockSpec(shape, lambda i, *_: (0,) * len(shape))
 
@@ -364,57 +431,64 @@
             device_id_type=MESH,
         )
 
-    swap = remote(src.at[1 - core], first, core_sems, 0, 0, (partner, me))
-    swap.start()
-    swap.wait()
-
-    def add_first(j, carry):
-        total = src[core, j].astype(jnp.float32) + first[j].astype(jnp.float32)
-        first_sum[j] = total.astype(jnp.bfloat16)
-        return carry
-
-    lax.fori_loop(0, halves * owners, add_first, 0)
-
-    def to_side(i, arriving):
-        other = lax.rem(side + i, halves)
+    def bucket_of(i):
+        return lax.rem(me + 1 + i, owners)
+
+    def swap(i):
+        bucket = bucket_of(i)
+        return remote(src.at[bucket, 1 - core], first.at[bucket], core_sems, i, i, (partner, me))
+
+    def to_side(i, n, arriving):
+        bucket = bucket_of(i)
+        other = lax.rem(side + n, halves)
         slot = other if arriving else side
         return remote(
-            first_sum.at[pl.ds(other * owners, owners)],
-            second.at[slot],
-            pair_sems, i, slot,
-            (other * 2 + core, me),
+            first_sum.at[bucket, other], second.at[slot, bucket], pair_sems,
+            n * owners + i, slot * owners + i, (other * 2 + core, me),
         )
-
-    for i in range(1, halves):
-        to_side(i, False).start()
-    for i in range(1, halves):
-        to_side(i, True).wait_recv()
-
-    def add_second(j, carry):
-        total = first_sum[side * owners + j].astype(jnp.float32)
-        for i in range(1, halves):
-            total = total + second[lax.rem(side + i, halves), j].astype(jnp.float32)
-        second_sum[j] = total.astype(jnp.bfloat16)
-        return carry
-
-    lax.fori_loop(0, owners, add_second, 0)
 
     def to_owner(i, arriving):
         other = owner_peer(i)
         slot = other if arriving else me
         return remote(second_sum.at[other], third.at[slot], row_sems, i, slot, (dp, other))
 
-    def send_owner(i, carry):
-        to_owner(i, False).start()
+    def start_swap(i, carry):
+        swap(i).start()
+        return carry
+
+    def add_first(i, carry):
+        bucket = bucket_of(i)
+        swap(i).wait_recv()
+        total = src[bucket, core].astype(jnp.float32) + first[bucket].astype(jnp.float32)
+        first_sum[bucket] = total.astype(jnp.bfloat16)
+        for n in range(1, halves):
+            to_side(i, n, False).start()
+        return carry
+
+    def add_second(i, carry):
+        bucket = bucket_of(i)
+        total = first_sum[bucket, side].astype(jnp.float32)
+        for n in range(1, halves):
+            to_side(i, n, True).wait_recv()
+            total = total + second[lax.rem(side + n, halves), bucket].astype(jnp.float32)
+        second_sum[bucket] = total.astype(jnp.bfloat16)
+        return carry
+
+    def add_and_send(i, carry):
+        add_second(i, carry)
+        to_owner(i + 1, False).start()
         return carry
 
     def wait_owner(i, carry):
         to_owner(i, True).wait_recv()
         return carry
 
-    lax.fori_loop(1, owners, send_owner, 0)
+    lax.fori_loop(0, owners, start_swap, 0)
+    lax.fori_loop(0, owners, add_first, 0)
+    lax.fori_loop(0, owners - 1, add_and_send, 0)
+    add_second(owners - 1, 0)
+    third[me] = second_sum[me]
     lax.fori_loop(1, owners, wait_owner, 0)
-    third[me] = second_sum[me]
     total = lax.fori_loop(
         1, owners, lambda i, t: t + third[i].astype(jnp.float32), third[0].astype(jnp.float32)
     )
@@ -446,8 +520,13 @@
         to_group(i, False).wait_send()
         return carry
 
-    for i in range(1, halves):
-        to_side(i, False).wait_send()
+    def sent_first(i, carry):
+        swap(i).wait_send()
+        for n in range(1, halves):
+            to_side(i, n, False).wait_send()
+        return carry
+
+    lax.fori_loop(0, owners, sent_first, 0)
     lax.fori_loop(1, owners, sent_owner, 0)
     lax.fori_loop(1, groups, sent_group, 0)
 
@@ -456,8 +535,7 @@
     groups, owners = lax.axis_size("dp"), lax.axis_size("bucket")
     halves = groups // 2
     rows = packed.shape[1] // groups
-    source = packed.reshape(owners, 2, halves, rows, LANES).transpose(1, 2, 0, 3, 4)
-    source = source.reshape(2, halves * owners, rows, LANES)
+    source = packed.reshape(owners, 2, halves, rows, LANES)
     kind = jnp.bfloat16
     return pl.pallas_call(
         functools.partial(reduce_kernel, groups, owners),
@@ -465,14 +543,14 @@
         in_specs=[pl.BlockSpec(memory_space=pltpu.VMEM)],
         out_specs=pl.BlockSpec(memory_space=pltpu.VMEM),
         scratch_shapes=[
-            pltpu.VMEM((halves * owners, rows, LANES), kind),
-            pltpu.VMEM((halves * owners, rows, LANES), kind),
+            pltpu.VMEM((owners, halves, rows, LANES), kind),
+            pltpu.VMEM((owners, halves, rows, LANES), kind),
             pltpu.VMEM((halves, owners, rows, LANES), kind),
             pltpu.VMEM((owners, rows, LANES), kind),
             pltpu.VMEM((owners, rows, LANES), kind),
             pltpu.VMEM((rows, LANES), kind),
-            pltpu.SemaphoreType.DMA((2, 1)),
-            pltpu.SemaphoreType.DMA((2, halves)),
+            pltpu.SemaphoreType.DMA((2, owners)),
+            pltpu.SemaphoreType.DMA((2, halves * owners)),
             pltpu.SemaphoreType.DMA((2, owners)),
             pltpu.SemaphoreType.DMA((2, groups)),
         ],
@@ -482,13 +560,8 @@
     )(source)
 
 
-def pick(array, index):
-    return array.at[index].get(mode="promise_in_bounds")
-
-
 def local(frames, lengths, owners, upstream, ln_gain, w_in, w_dw, bn_gain, bn_bias, w_out):
     loaders = lax.axis_size("bucket")
-    own_index = lax.axis_index("bucket")
     width = frames.shape[1]
     taps = w_dw.shape[1]
     slot_count = lengths.shape[1] // loaders
@@ -497,33 +570,26 @@
     own_rows = upstream.shape[0]
     blocks = width // LANES
     total_frames = float(own_rows * loaders * lax.axis_size("dp"))
-    lens_all = lengths[0].reshape(loaders, slot_count)
-    dest_all = owners[0].reshape(loaders, slot_count)
-    owner_ids = jnp.arange(loaders, dtype=jnp.int32)
-    onehot = (dest_all[:, :, None] == owner_ids[None, None, :]).astype(jnp.int32)
-    earlier = jnp.cumsum(onehot, axis=1) - onehot
-    ranking = jnp.sum(earlier * onehot, axis=2)
-    send_pos = dest_all * pair_count + ranking
-    my_pos = lax.dynamic_index_in_dim(send_pos, own_index, 0, keepdims=False)
-    my_lens = lax.dynamic_index_in_dim(lens_all, own_index, 0, keepdims=False)
-    slot_ids = jnp.arange(slot_count, dtype=jnp.int32)
-    send_order = jnp.sum(
-        jnp.where(my_pos[None, :] == slot_ids[:, None], slot_ids[None, :], 0), axis=1
-    )
-    pair_ids = jnp.arange(pair_count, dtype=jnp.int32)
-    to_me = (dest_all == own_index)[:, :, None] & (ranking[:, :, None] == pair_ids[None, None, :])
-    recv_lens = jnp.sum(jnp.where(to_me, lens_all[:, :, None], 0), axis=1).reshape(-1)
-    starts = jnp.cumsum(recv_lens) - recv_lens
-    position = jnp.arange(span, dtype=jnp.int32)
-    row_ids = jnp.arange(own_rows, dtype=jnp.int32)
-    reached = (starts[None, :] <= row_ids[:, None]).astype(jnp.int32)
-    row_slot = jnp.sum(reached, axis=1) - 1
-    row_start = jnp.max(reached * starts[None, :], axis=1)
-    packed_source = row_slot * span + row_ids - row_start
-    slot_target = jnp.minimum(starts[:, None] + position[None, :], own_rows - 1).reshape(-1)
-
-    outgoing = pick(upstream, slot_target).reshape(loaders, pair_count, span, width)
-    incoming = lax.all_to_all(outgoing, "bucket", split_axis=0, concat_axis=0, tiled=True)
+    stage_shape = pltpu.VMEM((blocks, own_rows + span, LANES), jnp.float32)
+    slot_shape = jax.ShapeDtypeStruct((slot_count, span, width), jnp.bfloat16)
+    in_vmem = pl.BlockSpec(memory_space=pltpu.VMEM)
+    in_smem = pl.BlockSpec(memory_space=pltpu.SMEM)
+    outgoing, meta = pl.pallas_call(
+        functools.partial(plan_kernel, slot_count),
+        in_specs=[in_smem, in_smem, in_vmem],
+        out_specs=[in_vmem, in_smem],
+        out_shape=[slot_shape, jax.ShapeDtypeStruct((3, slot_count), jnp.int32)],
+        scratch_shapes=[stage_shape, pltpu.SMEM((loaders,), jnp.int32)],
+        compiler_params=pltpu.CompilerParams(vmem_limit_bytes=VMEM_LIMIT),
+        name="plan",
+    )(lengths, owners, upstream)
+
+    def exchange(slots):
+        slots = slots.reshape(loaders, pair_count, span, width)
+        moved = lax.all_to_all(slots, "bucket", split_axis=0, concat_axis=0, tiled=True)
+        return moved.reshape(slot_count, span, width)
+
+    incoming = exchange(outgoing)
 
     group = 4
     steps = slot_count // group
@@ -557,23 +623,22 @@
             flops=2 * 10**9, bytes_accessed=4 * 10**7, transcendentals=0
         ),
         name="forward",
-    )(my_lens, frames, gain_row, w_in, w_taps)
+    )(meta, frames, gain_row, w_in, w_taps)
     totals = sum_everywhere(part, 0)
 
-    work_grad = pick(incoming.reshape(slot_count, span, width), my_pos).reshape(all_rows, width)
     out_rows, grad_bn, back_part, grad_wout = pl.pallas_call(
         functools.partial(middle_kernel, group, span, total_frames),
         grid_spec=pltpu.PrefetchScalarGridSpec(
             num_scalar_prefetch=1,
             grid=(steps,),
             in_specs=[
-                row_block, row_block, whole(sums_shape), whole((1, width)), whole((1, width)),
-                whole(w_out.shape),
+                row_block, whole(slot_shape.shape), whole(sums_shape), whole((1, width)),
+                whole((1, width)), whole(w_out.shape),
             ],
-            out_specs=[row_block, row_block, whole(sums_shape), whole(w_out.shape)],
+            out_specs=[whole(slot_shape.shape), row_block, whole(sums_shape), whole(w_out.shape)],
         ),
         out_shape=[
-            jax.ShapeDtypeStruct((all_rows, width), jnp.bfloat16),
+            slot_shape,
             jax.ShapeDtypeStruct((all_rows, width), jnp.float32),
             jax.ShapeDtypeStruct(sums_shape, jnp.float32),
             jax.ShapeDtypeStruct(w_out.shape, jnp.float32),
@@ -583,13 +648,11 @@
             flops=3 * 10**9, bytes_accessed=2 * 10**7, transcendentals=0
         ),
         name="middle",
-    )(my_lens, conv, work_grad, totals, bn_gain_row, bn_bias_row, w_out)
-
-    leaving = pick(out_rows.reshape(slot_count, span, width), send_order).reshape(
-        loaders, pair_count, span, width
-    )
-    arrived = lax.all_to_all(leaving, "bucket", split_axis=0, concat_axis=0, tiled=True)
+    )(meta, conv, incoming, totals, bn_gain_row, bn_bias_row, w_out)
+
     back_totals = sum_everywhere(back_part, 1)
+    leaving, back_totals = lax.optimization_barrier((out_rows, back_totals))
+    arrived = exchange(leaving)
 
     share = width // loaders
     packed_rows = (w_in.shape[1] // LANES + blocks + 1) * share
@@ -624,15 +687,24 @@
         ),
         name="backward",
     )(
-        my_lens, frames, conv, grad_bn, totals, back_totals, gain_row, bn_gain_row, w_in, w_taps,
+        meta, frames, conv, grad_bn, totals, back_totals, gain_row, bn_gain_row, w_in, w_taps,
         grad_wout,
     )
-    reduced = reduce_rows(packed, 2).reshape(-1, share, LANES).astype(jnp.float32)
-    out_frames = pick(arrived.reshape(slot_count * span, width), packed_source)
-    wide = w_in.shape[1] // LANES
-    grad_win = reduced[:wide].transpose(1, 0, 2).reshape(share, -1)
-    grad_wo = reduced[wide : wide + blocks].transpose(1, 0, 2).reshape(share, -1)
-    last = reduced[wide + blocks]
+    reduced = reduce_rows(packed, 2).reshape(-1, share, LANES)
+    out_frames, grad_win, grad_wo, last = pl.pallas_call(
+        finish_kernel,
+        in_specs=[in_smem, in_vmem, in_vmem],
+        out_specs=[in_vmem] * 4,
+        out_shape=[
+            jax.ShapeDtypeStruct((own_rows, width), jnp.bfloat16),
+            jax.ShapeDtypeStruct((share, w_in.shape[1]), jnp.float32),
+            jax.ShapeDtypeStruct((share, width), jnp.float32),
+            jax.ShapeDtypeStruct((share, LANES), jnp.float32),
+        ],
+        scratch_shapes=[stage_shape],
+        compiler_params=pltpu.CompilerParams(vmem_limit_bytes=VMEM_LIMIT),
+        name="finish",
+    )(meta, arrived, reduced)
     flat_back = back_totals.reshape(2, width)
     return (
         out_frames,

time: 207 us -> 157 us (0.76)
  Pallas kernels: 158 us -> 129 us
  local copies, waits for them, and re-layouts: 30.5 us -> 15.8 us
  other arithmetic: 5.11 us -> 0 us
    pallas_call x2, Pallas kernels: 67.6 us -> 34.6 us  [sum_everywhere(): pl.pallas_call(functools.partial(sum_kernel, groups, owners), out_shape=j...]
    gather x4 -> x0, local copies, waits for them, and re-layouts: 15.7 us -> none  [pick(): return array.at[index].get(mode='promise_in_bounds')]
    pallas_call x0 -> x2, Pallas kernels: none -> 8.14 us  [the longest x1 6.11 us: local(): pl.pallas_call(functools.partial(plan_kernel, slot_count), in_specs=[in_s...]
    unnamed x42 -> x43, local copies, waits for them, and re-layouts: 9.05 us -> 14.5 us
    pallas_call x1, Pallas kernels: 31.4 us -> 26.5 us  [reduce_rows(): pl.pallas_call(functools.partial(reduce_kernel, groups, owners), out_shap...]
    unnamed x2 -> x0, other arithmetic: 2.68 us -> none
    reshape x3 -> x0, local copies, waits for them, and re-layouts: 2.68 us -> none  [the longest x1 1.3 us: reduce_rows(): packed.reshape(owners, 2, halves, rows, LANES).transpose(1, 2, 0, 3, 4)]
  transfers between devices with their start and end apart: 2 -> 2, of which waited for: 0 -> 0; matrix products, arithmetic and copies ran while one was open for 3% -> 0% of each run, Pallas kernels for 73% -> 65%
where the time goes in v2:
time: 157 us; the launch traced here: 156 us
  Pallas kernels  129 us (82%)
  local copies, waits for them, and re-layouts  15.8 us (10%)
  starting transfers between devices  10.4 us (7%)
    pallas_call x2, Pallas kernels, sum_everywhere(): pl.pallas_call(functools.partial(sum_kernel, groups, owners), out_shape=j...  34.6 us
    pallas_call x1, Pallas kernels, local(): pl.pallas_call(functools.partial(backward_kernel, group, span, taps, tota...  34.6 us
    pallas_call x1, Pallas kernels, reduce_rows(): pl.pallas_call(functools.partial(reduce_kernel, groups, owners), out_shap...  26.5 us
    pallas_call x1, Pallas kernels, local(): pl.pallas_call(functools.partial(forward_kernel, group, span, taps), grid...  15.5 us
    unnamed x43, local copies, waits for them, and re-layouts  14.5 us
    all_to_all x2, starting transfers between devices, exchange(): lax.all_to_all(slots, 'bucket', split_axis=0, concat_axis=0, tiled=True)  10.4 us
    pallas_call x1, Pallas kernels, local(): pl.pallas_call(functools.partial(middle_kernel, group, span, total_frames...  9.28 us
    pallas_call x1, Pallas kernels, local(): pl.pallas_call(functools.partial(plan_kernel, slot_count), in_specs=[in_s...  6.11 us
  transfers between devices with their start and end apart: 2, of which 0 were waited for; matrix products, arithmetic and copies ran while one was open for 0% of the time, Pallas kernels for 65%

profile of v2, /device:TPU:1, one launch (start us, length us, event | category | flops | bytes accessed | tf_op | source)
XLA Modules:
  0.0 155.7 jit_solution(11315864505115166673)
XLA Ops:
  0.6 1.1 copy-done.2
  1.8 0.7 copy-done.8
  2.4 0.7 copy-done.9
  3.1 6.1 %plan.1 = (bf16[32,48,512]{2,1,0:T(8,128)(2,1)}, s32[3,32]{1,0:T(4,128)S(1)}) custom-call(s32[1,256]{1,0:T(1,128)S(1)} %copy-done.8, s32[1,256]{1,0:T(1,128)S(1)} %copy-done.9, bf16[768,512]{1,0:T(8,128)(2,1)S(1)} %copy-done.2), custom_call_target="tpu_custom_call" | custom-call | tf_op jit(solution)/shard_map/plan/pallas_call | solution.py:577
  9.2 0.0 copy-start.20
  9.3 0.0 copy-start.10
  9.3 0.0 copy-start.15
  9.3 6.5 %all-to-all-start = ((bf16[8,4,48,512]{3,2,1,0:T(8,128)(2,1)}), bf16[8,4,48,512]{3,2,1,0:T(8,128)(2,1)S(1)}, u32[]{:S(2)}, u32[]{:S(2)}) async-start(bf16[8,4,48,512]{3,2,1,0:T(8,128)(2,1)} %bitcast.2), calls=%async_computation | async-start | bytes 3145728 | tf_op jit(solution)/shard_map/all_to_all | solution.py:589
  15.8 1.2 copy-done.11
  17.0 15.5 %forward.1 = (f32[1536,512]{1,0:T(8,128)S(1)}, f32[8,128]{1,0:T(8,128)S(1)}) custom-call(s32[3,32]{1,0:T(4,128)S(1)} %get-tuple-element.24.lens_ref.meta_ref, bf16[1536,512]{1,0:T(8,128)(2,1)S(1)} %copy-done.10, f32[1,512]{1,0:T(1,128)S(1)} %bitcast.21, bf16[512,1024]{1,0:T(8,128)(2,1)S(1)} %copy-done.11, f32[32,512]{1,0:T(8,128)S(1)} %pad.4.w_dw_ref), custom_call_target="tpu_custom_call" | custom-call | flops 2000000000 | bytes 40000000 | tf_op jit(solution)/shard_map/forward/pallas_call | solution.py:608
  32.6 0.0 copy-start.7
  32.6 0.6 copy-done.7
  33.2 1.6 %copy-done.17 = f32[1536,512]{1,0:T(8,128)} copy-done((f32[1536,512]{1,0:T(8,128)}, f32[1536,512]{1,0:T(8,128)S(1)}, u32[]{:S(2)}) %copy-start.17) | copy-done | bytes 3145752
  34.8 24.3 %sum_everywhere_0.1.total_ref = f32[8,128]{1,0:T(8,128)} custom-call(f32[8,128]{1,0:T(8,128)} %copy-done.7), custom_call_target="tpu_custom_call" | custom-call | flops 1000000 | bytes 20000000 | tf_op jit(solution)/shard_map/sum_everywhere_0/pallas_call | solution.py:381
  59.2 0.7 copy-done.4
  59.8 1.0 copy-done.13
  60.9 9.3 %middle.1 = (bf16[32,48,512]{2,1,0:T(8,128)(2,1)}, f32[1536,512]{1,0:T(8,128)}, f32[8,128]{1,0:T(8,128)S(1)}, f32[512,512]{1,0:T(8,128)S(1)}) custom-call(s32[3,32]{1,0:T(4,128)S(1)} %get-tuple-element.24.lens_ref.meta_ref, f32[1536,512]{1,0:T(8,128)} %copy-done.17, bf16[32,48,512]{2,1,0:T(8,128)(2,1)S(1)} %bitcast.17, f32[8,128]{1,0:T(8,128)S(1)} %copy-done.4, ...), custom_call_target="tpu_custom_call" | custom-call | flops 3000000000 | bytes 20000000 | tf_op jit(solution)/shard_map/middle/pallas_call | solution.py:629
  70.1 0.6 copy-done.6
  70.7 1.0 copy-done.18
  71.7 10.3 %sum_everywhere_1.1.back_ref = f32[8,128]{1,0:T(8,128)} custom-call(f32[8,128]{1,0:T(8,128)} %copy-done.6), custom_call_target="tpu_custom_call" | custom-call | flops 1000000 | bytes 20000000 | tf_op jit(solution)/shard_map/sum_everywhere_1/pallas_call | solution.py:381
  82.1 3.9 %all-to-all-start.1 = ((bf16[8,4,48,512]{3,2,1,0:T(8,128)(2,1)}), bf16[8,4,48,512]{3,2,1,0:T(8,128)(2,1)S(1)}, u32[]{:S(2)}, u32[]{:S(2)}) async-start(bf16[8,4,48,512]{3,2,1,0:T(8,128)(2,1)} %bitcast.6), calls=%async_computation.1 | async-start | bytes 3145728 | tf_op jit(solution)/shard_map/all_to_all | solution.py:589
  86.0 0.0 copy-start.12
  86.0 1.2 copy-done.12
  87.2 1.2 copy-done.19
  88.5 34.6 %backward.1 = (bf16[1536,512]{1,0:T(8,128)(2,1)}, bf16[8,832,128]{2,1,0:T(8,128)(2,1)S(1)}) custom-call(s32[3,32]{1,0:T(4,128)S(1)} %get-tuple-element.24.lens_ref.meta_ref, bf16[1536,512]{1,0:T(8,128)(2,1)S(1)} %copy-done.10, f32[1536,512]{1,0:T(8,128)} %copy-done.17, f32[1536,512]{1,0:T(8,128)} %get-tuple-element.31.grad_bn_ref, f32[8,128]{1,0:T(8,128)S(1)} %copy-done.5, ...), custom_call_target="tpu_custom_call" | custom-call | flops 6000000000 | bytes 80000000 | tf_op jit(solution)/shard_map/backward/pallas_call | solution.py:659
  123.0 1.2 copy-done
  124.2 26.5 %reduce_rows.1 = bf16[4,208,128]{2,1,0:T(8,128)(2,1)} custom-call(bf16[8,2,2,208,128]{4,3,2,1,0:T(8,128)(2,1)} %bitcast.16), custom_call_target="tpu_custom_call" | custom-call | flops 10000000 | bytes 60000000 | tf_op jit(solution)/shard_map/reduce_rows/pallas_call | solution.py:540
  150.8 0.6 slice_bitcast_fusion
  151.3 0.9 copy-done.1
  152.3 2.0 %finish.1 = (bf16[768,512]{1,0:T(8,128)(2,1)}, f32[64,1024]{1,0:T(8,128)}, f32[64,512]{1,0:T(8,128)}, f32[64,128]{1,0:T(8,128)S(1)}) custom-call(s32[3,32]{1,0:T(4,128)S(1)} %get-tuple-element.24.lens_ref.meta_ref, bf16[32,48,512]{2,1,0:T(8,128)(2,1)S(1)} %bitcast.15, bf16[13,64,128]{2,1,0:T(8,128)(2,1)S(1)} %bitcast.18), custom_call_target="tpu_custom_call" | custom-call | tf_op jit(solution)/shard_map/finish/pallas_call | solution.py:694
  154.3 0.7 slice_reduce_fusion
  155.0 0.7 copy.19
  (26 shorter events, 0.1 us)
Async XLA Ops:
  0.6 1.1 copy-start.2
  1.8 0.7 copy-start.8
  2.4 0.7 copy-start.9
  9.2 6.5 %copy-start.20 = (f32[512,31]{0,1:T(8,128)S(1)}, f32[512,31]{0,1:T(8,128)}, u32[]{:S(2)}) copy-start(f32[512,31]{0,1:T(8,128)} %param.16) | copy-start | bytes 190468
  9.3 6.5 %copy-start.10 = (bf16[1536,512]{1,0:T(8,128)(2,1)S(1)}, bf16[1536,512]{1,0:T(8,128)(2,1)}, u32[]{:S(2)}) copy-start(bf16[1536,512]{1,0:T(8,128)(2,1)} %frames_ref.3) | copy-start | bytes 4718596
  9.3 6.5 %copy-start.15 = (f32[512]{0:T(512)S(1)}, f32[512]{0:T(512)}, u32[]{:S(2)}) copy-start(f32[512]{0:T(512)} %param.14) | copy-start | bytes 6148
  9.3 49.8 %all-to-all-start = ((bf16[8,4,48,512]{3,2,1,0:T(8,128)(2,1)}), bf16[8,4,48,512]{3,2,1,0:T(8,128)(2,1)S(1)}, u32[]{:S(2)}, u32[]{:S(2)}) async-start(bf16[8,4,48,512]{3,2,1,0:T(8,128)(2,1)} %bitcast.2), calls=%async_computation | async-start | bytes 3145728 | tf_op jit(solution)/shard_map/all_to_all | solution.py:589
  15.8 1.2 copy-start.11
  17.0 42.1 %copy-start.14 = (f32[512]{0:T(512)S(1)}, f32[512]{0:T(512)}, u32[]{:S(2)}) copy-start(f32[512]{0:T(512)} %param.18) | copy-start | bytes 6148
  17.0 42.1 %copy-start.16 = (f32[512]{0:T(512)S(1)}, f32[512]{0:T(512)}, u32[]{:S(2)}) copy-start(f32[512]{0:T(512)} %param.17) | copy-start | bytes 6148
  32.6 0.6 copy-start.7
  33.2 1.6 %copy-start.17 = (f32[1536,512]{1,0:T(8,128)}, f32[1536,512]{1,0:T(8,128)S(1)}, u32[]{:S(2)}) copy-start(f32[1536,512]{1,0:T(8,128)S(1)} %get-tuple-element.25.conv_ref) | copy-start | bytes 9437188
  59.1 0.7 copy-start.4
  59.8 1.0 copy-start.13
  70.1 0.6 copy-start.6
  70.7 1.0 copy-start.18
  82.1 3.9 %copy-start.3 = (f32[8,128]{1,0:T(8,128)S(1)}, f32[8,128]{1,0:T(8,128)}, u32[]{:S(2)}) copy-start(f32[8,128]{1,0:T(8,128)} %sum_everywhere_1.1.back_ref) | copy-start | bytes 12292
  82.1 3.9 %copy-start.5 = (f32[8,128]{1,0:T(8,128)S(1)}, f32[8,128]{1,0:T(8,128)}, u32[]{:S(2)}) copy-start(f32[8,128]{1,0:T(8,128)} %sum_everywhere_0.1.total_ref) | copy-start | bytes 12292
  82.1 69.3 %all-to-all-start.1 = ((bf16[8,4,48,512]{3,2,1,0:T(8,128)(2,1)}), bf16[8,4,48,512]{3,2,1,0:T(8,128)(2,1)S(1)}, u32[]{:S(2)}, u32[]{:S(2)}) async-start(bf16[8,4,48,512]{3,2,1,0:T(8,128)(2,1)} %bitcast.6), calls=%async_computation.1 | async-start | bytes 3145728 | tf_op jit(solution)/shard_map/all_to_all | solution.py:589
  86.0 1.2 copy-start.12
  87.2 1.2 copy-start.19
  123.0 1.2 copy-start
  151.3 0.9 copy-start.1

commit v3 on v2

--- a/solution.py
+++ b/solution.py
@@ -11,7 +11,7 @@
 LANES = 128
 SUB = 8
 MESH = pl.DeviceIdType.MESH
-VMEM_LIMIT = 48 << 20
+VMEM_LIMIT = 24 << 20
 
 
 def lane(c):
@@ -46,42 +46,52 @@
     h = (normed * gain).astype(jnp.bfloat16)
     projected = jnp.dot(h, w_in, preferred_element_type=jnp.float32)
     half = projected.shape[1] // 2
-    return normed, inverse, h, projected[:, :half], jax.nn.sigmoid(projected[:, half:])
-
-
-def shifted_sum(padded, weight, span, taps):
+    return normed, inverse, projected[:, :half], jax.nn.sigmoid(projected[:, half:])
+
+
+def shifted_sum(frame, weight, span, taps):
+    lead = (taps + 1) // 2 // SUB
+    count = span // SUB
+    tiles = [frame[i * SUB : (i + 1) * SUB] for i in range(count)]
     total = None
     for residue in range(SUB):
-        part = None
-        for k in range(residue, taps + 1, SUB):
-            if k == 0:
-                continue
-            term = padded[k - residue : k - residue + span + SUB] * weight(k)
-            part = term if part is None else part + term
+        shifts = [k for k in range(residue, taps + 1, SUB) if k > 0]
+        weights = {k: jnp.broadcast_to(weight(k), (SUB, LANES)) for k in shifts}
+        parts = []
+        for i in range(count + 1 if residue else count):
+            part = None
+            for k in shifts:
+                at = (k - residue) // SUB + i - lead
+                if 0 <= at < count:
+                    term = tiles[at] * weights[k]
+                    part = term if part is None else part + term
+            parts.append(jnp.zeros((SUB, LANES), jnp.float32) if part is None else part)
+        moved = jnp.concatenate(parts, axis=0)
         if residue:
-            part = pltpu.roll(part, span + SUB - residue, 0)
-        part = part[:span]
-        total = part if total is None else total + part
+            moved = pltpu.roll(moved, span + SUB - residue, 0)[:span]
+        total = moved if total is None else total + moved
     return total
 
 
 def forward_kernel(group, span, taps, lens_ref, frames_ref, gain_ref, w_in_ref, w_dw_ref,
-                   conv_ref, sums_ref, padded):
+                   conv_ref, sums_ref, normed_ref, inverse_ref, linear_ref, gate_ref, padded):
     step = pl.program_id(0)
     blocks = conv_ref.shape[1] // LANES
-    edge = (padded.shape[2] - span) // 2
 
     @pl.when(step == 0)
     def _():
-        padded[...] = jnp.zeros_like(padded)
         sums_ref[...] = jnp.zeros_like(sums_ref)
 
     masks = live_rows(lens_ref, step * group, group, span, conv_ref.shape[1])
-    _, _, _, linear, gate = project(frames_ref[...], gain_ref[...], w_in_ref[...])
+    normed, inverse, linear, gate = project(frames_ref[...], gain_ref[...], w_in_ref[...])
+    normed_ref[...] = normed
+    inverse_ref[...] = jnp.broadcast_to(inverse, inverse_ref.shape)
+    linear_ref[...] = linear
+    gate_ref[...] = gate
     gated = keep_live(linear * gate, masks, span).astype(jnp.bfloat16).astype(jnp.float32)
     for u in range(group):
         for c in range(blocks):
-            padded[u, c, edge : edge + span] = gated[u * span : (u + 1) * span, lane(c)]
+            padded[u, c] = gated[u * span : (u + 1) * span, lane(c)]
 
     def one(u, carry):
         live = lax.broadcasted_iota(jnp.int32, (span, LANES), 0) < lens_ref[0, step * group + u]
@@ -147,27 +157,26 @@
         sums_ref[blocks + c : blocks + c + 1] += gain_row[:, lane(c)]
 
 
-def backward_kernel(group, span, taps, total_frames, lens_ref, frames_ref, conv_ref, grad_bn_ref,
+def backward_kernel(group, span, taps, total_frames, lens_ref, normed_ref, inverse_ref,
+                    linear_ref, gate_ref, conv_ref, grad_bn_ref,
                     total_ref, back_ref, gain_ref, bn_gain_ref, w_in_ref, w_dw_ref, wout_ref,
                     grad_frames_ref, packed_ref, padded, grad_pad, gated_grad, w_acc, win_acc,
                     ln_acc, flat):
     step = pl.program_id(0)
     width = conv_ref.shape[1]
     blocks = width // LANES
-    edge = (padded.shape[2] - span) // 2
+    count = span // SUB
+    lead = (taps + 1) // 2 // SUB
 
     @pl.when(step == 0)
     def _():
-        padded[...] = jnp.zeros_like(padded)
-        grad_pad[...] = jnp.zeros_like(grad_pad)
         w_acc[...] = jnp.zeros_like(w_acc)
         win_acc[...] = jnp.zeros_like(win_acc)
         ln_acc[...] = jnp.zeros_like(ln_acc)
 
     masks = live_rows(lens_ref, step * group, group, span, width)
     w_in = w_in_ref[...]
-    normed, inverse, h, linear, gate = project(frames_ref[...], gain_ref[...], w_in)
-    gated = keep_live(linear * gate, masks, span).astype(jnp.bfloat16).astype(jnp.float32)
+    gated = keep_live(linear_ref[...] * gate_ref[...], masks, span).astype(jnp.bfloat16).astype(jnp.float32)
     bn_normed, bn_inverse = batch_norm(total_ref, conv_ref[...], total_frames, blocks)
     back = back_ref[...]
     bias_mean = row_of(back, 0, blocks) / total_frames
@@ -180,8 +189,8 @@
     for u in range(group):
         for c in range(blocks):
             rows = slice(u * span, (u + 1) * span)
-            padded[u, c, edge : edge + span] = gated[rows, lane(c)]
-            grad_pad[u, c, edge : edge + span] = grad_conv[rows, lane(c)]
+            padded[u, c] = gated[rows, lane(c)]
+            grad_pad[u, c] = grad_conv[rows, lane(c)]
 
     def one(u, carry):
         start = pl.multiple_of(u * span, SUB)
@@ -190,7 +199,8 @@
             gated_grad[pl.ds(start, span), lane(c)] = shifted_sum(
                 grads, lambda k: w_dw_ref[taps - k : taps - k + 1, lane(c)], span, taps
             )
-            inner = grads[edge - SUB : edge + span + SUB]
+            blank = jnp.zeros((SUB, LANES), jnp.float32)
+            inner = jnp.concatenate([blank, grads, blank], axis=0)
             frame = padded[u, c]
             for residue in range(SUB):
                 moved = inner if residue == 0 else pltpu.roll(inner, residue, 0)
@@ -198,16 +208,22 @@
                 for k in range(residue, taps + 1, SUB):
                     if k == 0:
                         continue
-                    term = moved * frame[k - residue : k - residue + span + SUB]
-                    part = term[:SUB]
-                    for i in range(1, span // SUB + 1):
-                        part = part + term[i * SUB : (i + 1) * SUB]
+                    part = None
+                    for i in range(count + 1 if residue else count):
+                        at = (k - residue) // SUB + i - lead
+                        if 0 <= at < count:
+                            tile = frame[at * SUB : (at + 1) * SUB]
+                            term = moved[i * SUB : (i + 1) * SUB] * tile
+                            part = term if part is None else part + term
                     w_acc[c, k - 1] += part
         return carry
 
     lax.fori_loop(0, group, one, 0)
 
     grad_gated = keep_live(gated_grad[...], masks, span)
+    linear, gate = linear_ref[...], gate_ref[...]
+    normed, inverse = normed_ref[...], inverse_ref[:, :1]
+    h = (normed * gain_ref[...]).astype(jnp.bfloat16)
     left = grad_gated * gate
     grad_a = jnp.concatenate(
         [left.astype(jnp.bfloat16), (left * linear * (1.0 - gate)).astype(jnp.bfloat16)], axis=1
@@ -388,7 +404,9 @@
             pltpu.SemaphoreType.DMA((count,)),
             pltpu.SemaphoreType.DMA((count,)),
         ],
-        compiler_params=pltpu.CompilerParams(collective_id=collective_id, has_side_effects=True),
+        compiler_params=pltpu.CompilerParams(
+            collective_id=collective_id, has_side_effects=True, vmem_limit_bytes=4 << 20
+        ),
         cost_estimate=pl.CostEstimate(flops=10**6, bytes_accessed=2 * 10**7, transcendentals=0),
         name="sum_everywhere_%d" % collective_id,
     )(part)
@@ -554,10 +572,16 @@
             pltpu.SemaphoreType.DMA((2, owners)),
             pltpu.SemaphoreType.DMA((2, groups)),
         ],
-        compiler_params=pltpu.CompilerParams(collective_id=collective_id, has_side_effects=True),
+        compiler_params=pltpu.CompilerParams(
+            collective_id=collective_id, has_side_effects=True, vmem_limit_bytes=16 << 20
+        ),
         cost_estimate=pl.CostEstimate(flops=10**7, bytes_accessed=6 * 10**7, transcendentals=0),
         name="reduce_rows",
     )(source)
+
+
+def in_hbm(array):
+    return pltpu.with_memory_space_constraint(array, pltpu.HBM)
 
 
 def local(frames, lengths, owners, upstream, ln_gain, w_in, w_dw, bn_gain, bn_bias, w_out):
@@ -594,7 +618,6 @@
     group = 4
     steps = slot_count // group
     rows = group * span
-    edge = (taps + 1) // 2
     row_block = pl.BlockSpec((rows, width), lambda i, *_: (i, 0))
     all_rows = slot_count * span
     gain_row, bn_gain_row, bn_bias_row = ln_gain[None], bn_gain[None], bn_bias[None]
@@ -603,20 +626,28 @@
     params = pltpu.CompilerParams(
         dimension_semantics=("arbitrary",), vmem_limit_bytes=VMEM_LIMIT
     )
-    padded_shape = pltpu.VMEM((group, blocks, span + 2 * edge, LANES), jnp.float32)
-
-    conv, part = pl.pallas_call(
+    padded_shape = pltpu.VMEM((group, blocks, span, LANES), jnp.float32)
+
+    thin_block = pl.BlockSpec((rows, LANES), lambda i, *_: (i, 0))
+    tall = pltpu.HBM((all_rows, width), jnp.float32)
+    conv, part, normed, inverse, linear, gate = pl.pallas_call(
         functools.partial(forward_kernel, group, span, taps),
         grid_spec=pltpu.PrefetchScalarGridSpec(
             num_scalar_prefetch=1,
             grid=(steps,),
             in_specs=[row_block, whole((1, width)), whole(w_in.shape), whole(w_taps.shape)],
-            out_specs=[row_block, whole(sums_shape)],
+            out_specs=[
+                row_block, whole(sums_shape), row_block, thin_block, row_block, row_block
+            ],
             scratch_shapes=[padded_shape],
         ),
         out_shape=[
-            jax.ShapeDtypeStruct((all_rows, width), jnp.float32),
+            tall,
             jax.ShapeDtypeStruct(sums_shape, jnp.float32),
+            tall,
+            pltpu.HBM((all_rows, LANES), jnp.float32),
+            tall,
+            tall,
         ],
         compiler_params=params,
         cost_estimate=pl.CostEstimate(
@@ -639,16 +670,16 @@
         ),
         out_shape=[
             slot_shape,
-            jax.ShapeDtypeStruct((all_rows, width), jnp.float32),
+            tall,
             jax.ShapeDtypeStruct(sums_shape, jnp.float32),
-            jax.ShapeDtypeStruct(w_out.shape, jnp.float32),
+            pltpu.HBM(w_out.shape, jnp.float32),
         ],
         compiler_params=params,
         cost_estimate=pl.CostEstimate(
             flops=3 * 10**9, bytes_accessed=2 * 10**7, transcendentals=0
         ),
         name="middle",
-    )(meta, conv, incoming, totals, bn_gain_row, bn_bias_row, w_out)
+    )(meta, in_hbm(conv), incoming, totals, bn_gain_row, bn_bias_row, w_out)
 
     back_totals = sum_everywhere(back_part, 1)
     leaving, back_totals = lax.optimization_barrier((out_rows, back_totals))
@@ -662,7 +693,8 @@
             num_scalar_prefetch=1,
             grid=(steps,),
             in_specs=[
-                row_block, row_block, row_block, whole(sums_shape), whole(sums_shape),
+                row_block, thin_block, row_block, row_block, row_block, row_block,
+                whole(sums_shape), whole(sums_shape),
                 whole((1, width)), whole((1, width)), whole(w_in.shape), whole(w_taps.shape),
                 whole(w_out.shape),
             ],
@@ -687,8 +719,8 @@
         ),
         name="backward",
     )(
-        meta, frames, conv, grad_bn, totals, back_totals, gain_row, bn_gain_row, w_in, w_taps,
-        grad_wout,
+        meta, *map(in_hbm, (normed, inverse, linear, gate, conv, grad_bn)), totals, back_totals, gain_row, bn_gain_row, w_in, w_taps,
+        in_hbm(grad_wout),
     )
     reduced = reduce_rows(packed, 2).reshape(-1, share, LANES)
     out_frames, grad_win, grad_wo, last = pl.pallas_call(

time: 157 us -> 141 us (0.90)
  local copies, waits for them, and re-layouts: 15.8 us -> 6.74 us
  Pallas kernels: 129 us -> 122 us
    unnamed x43 -> x23, local copies, waits for them, and re-layouts: 14.5 us -> 5.45 us
    pallas_call x1, Pallas kernels: 34.6 us -> 29.1 us  [local(): pl.pallas_call(functools.partial(backward_kernel, group, span, taps, tota...]
    pallas_call x1, Pallas kernels: 26.5 us -> 24.3 us  [reduce_rows(): pl.pallas_call(functools.partial(reduce_kernel, groups, owners), out_shap...]
  transfers between devices with their start and end apart: 2 -> 2, of which waited for: 0 -> 0; matrix products, arithmetic and copies ran while one was open for 0% -> 0% of each run, Pallas kernels for 65% -> 68%
where the time goes in v3:
time: 141 us; the launch traced here: 140 us
  Pallas kernels  122 us (87%)
  starting transfers between devices  10.4 us (7%)
  local copies, waits for them, and re-layouts  6.74 us (5%)
    pallas_call x2, Pallas kernels, sum_everywhere(): pl.pallas_call(functools.partial(sum_kernel, groups, owners), out_shape=j...  35.7 us
    pallas_call x1, Pallas kernels, local(): pl.pallas_call(functools.partial(backward_kernel, group, span, taps, tota...  29.1 us
    pallas_call x1, Pallas kernels, reduce_rows(): pl.pallas_call(functools.partial(reduce_kernel, groups, owners), out_shap...  24.3 us
    pallas_call x1, Pallas kernels, local(): pl.pallas_call(functools.partial(forward_kernel, group, span, taps), grid...  15.1 us
    all_to_all x2, starting transfers between devices, exchange(): lax.all_to_all(slots, 'bucket', split_axis=0, concat_axis=0, tiled=True)  10.4 us
    pallas_call x1, Pallas kernels, local(): pl.pallas_call(functools.partial(middle_kernel, group, span, total_frames...  9.64 us
    pallas_call x1, Pallas kernels, local(): pl.pallas_call(functools.partial(plan_kernel, slot_count), in_specs=[in_s...  6.11 us
    unnamed x23, local copies, waits for them, and re-layouts  5.45 us
  transfers between devices with their start and end apart: 2, of which 0 were waited for; matrix products, arithmetic and copies ran while one was open for 0% of the time, Pallas kernels for 68%

profile of v3, /device:TPU:1, one launch (start us, length us, event | category | flops | bytes accessed | tf_op | source)
XLA Modules:
  0.0 139.9 jit_solution(16222740089104792042)
XLA Ops:
  0.6 0.0 copy-start
  0.6 1.1 copy-done
  1.8 0.7 copy-done.1
  2.4 0.7 copy-done.2
  3.1 6.1 %plan.1 = (bf16[32,48,512]{2,1,0:T(8,128)(2,1)}, s32[3,32]{1,0:T(4,128)S(1)}) custom-call(s32[1,256]{1,0:T(1,128)S(1)} %copy-done.1, s32[1,256]{1,0:T(1,128)S(1)} %copy-done.2, bf16[768,512]{1,0:T(8,128)(2,1)S(1)} %copy-done), custom_call_target="tpu_custom_call" | custom-call | tf_op jit(solution)/shard_map/plan/pallas_call | solution.py:601
  9.2 0.0 copy-start.10
  9.3 0.0 copy-start.3
  9.3 0.0 copy-start.8
  9.3 6.5 %all-to-all-start = ((bf16[8,4,48,512]{3,2,1,0:T(8,128)(2,1)}), bf16[8,4,48,512]{3,2,1,0:T(8,128)(2,1)S(1)}, u32[]{:S(2)}, u32[]{:S(2)}) async-start(bf16[8,4,48,512]{3,2,1,0:T(8,128)(2,1)} %bitcast.2), calls=%async_computation | async-start | bytes 3145728 | tf_op jit(solution)/shard_map/all_to_all | solution.py:613
  15.8 0.0 copy-done.10
  15.8 0.0 copy-done.3
  15.8 0.0 copy-done.8
  15.8 0.0 copy-start.4
  15.8 1.2 copy-done.4
  17.0 15.1 %forward.1 = (f32[1536,512]{1,0:T(8,128)}, f32[8,128]{1,0:T(8,128)S(1)}, f32[1536,512]{1,0:T(8,128)}, f32[1536,128]{1,0:T(8,128)}, f32[1536,512]{1,0:T(8,128)}, /*index=5*/f32[1536,512]{1,0:T(8,128)}) custom-call(s32[3,32]{1,0:T(4,128)S(1)} %get-tuple-element.28.lens_ref.meta_ref, bf16[1536,512]{1,0:T(8,128)(2,1)S(1)} %copy-done.3, f32[1,512]{1,0:T(1,128)S(1)} %bitcast.21, ...), custom_call_target="tpu_custom_call" | custom-call | flops 2000000000 | bytes 40000000 | tf_op jit(solution)/shard_map/forward/pallas_call | solution.py:633
  32.1 26.4 %sum_everywhere_0.1.total_ref = f32[8,128]{1,0:T(8,128)S(1)} custom-call(f32[8,128]{1,0:T(8,128)S(1)} %get-tuple-element.31.part_ref), custom_call_target="tpu_custom_call" | custom-call | flops 1000000 | bytes 20000000 | tf_op jit(solution)/shard_map/sum_everywhere_0/pallas_call | solution.py:397
  58.5 0.0 all-to-all-done
  58.5 0.0 copy-done.7
  58.5 0.0 copy-done.9
  58.5 0.0 copy-start.6
  58.6 1.0 copy-done.6
  59.6 9.6 %middle.1 = (bf16[32,48,512]{2,1,0:T(8,128)(2,1)}, f32[1536,512]{1,0:T(8,128)}, f32[8,128]{1,0:T(8,128)S(1)}, f32[512,512]{1,0:T(8,128)}) custom-call(s32[3,32]{1,0:T(4,128)S(1)} %get-tuple-element.28.lens_ref.meta_ref, f32[1536,512]{1,0:T(8,128)} %get-tuple-element.29.conv_ref, bf16[32,48,512]{2,1,0:T(8,128)(2,1)S(1)} %bitcast.17, ...), custom_call_target="tpu_custom_call" | custom-call | flops 3000000000 | bytes 20000000 | tf_op jit(solution)/shard_map/middle/pallas_call | solution.py:660
  69.2 9.3 %sum_everywhere_1.1.back_ref = f32[8,128]{1,0:T(8,128)S(1)} custom-call(f32[8,128]{1,0:T(8,128)S(1)} %get-tuple-element.33.part_ref), custom_call_target="tpu_custom_call" | custom-call | flops 1000000 | bytes 20000000 | tf_op jit(solution)/shard_map/sum_everywhere_1/pallas_call | solution.py:397
  78.6 3.9 %all-to-all-start.1 = ((bf16[8,4,48,512]{3,2,1,0:T(8,128)(2,1)}), bf16[8,4,48,512]{3,2,1,0:T(8,128)(2,1)S(1)}, u32[]{:S(2)}, u32[]{:S(2)}) async-start(bf16[8,4,48,512]{3,2,1,0:T(8,128)(2,1)} %bitcast.6), calls=%async_computation.1 | async-start | bytes 3145728 | tf_op jit(solution)/shard_map/all_to_all | solution.py:613
  82.4 0.0 copy-done.5
  82.4 29.1 %backward.1 = (bf16[1536,512]{1,0:T(8,128)(2,1)}, bf16[8,832,128]{2,1,0:T(8,128)(2,1)S(1)}) custom-call(s32[3,32]{1,0:T(4,128)S(1)} %get-tuple-element.28.lens_ref.meta_ref, f32[1536,512]{1,0:T(8,128)} %get-tuple-element.35.normed_ref, f32[1536,128]{1,0:T(8,128)} %get-tuple-element.36.inverse_ref, f32[1536,512]{1,0:T(8,128)} %get-tuple-element.37.linear_ref, ...), custom_call_target="tpu_custom_call" | custom-call | flops 6000000000 | bytes 80000000 | tf_op jit(solution)/shard_map/backward/pallas_call | solution.py:690
  111.6 24.3 %reduce_rows.1 = bf16[4,208,128]{2,1,0:T(8,128)(2,1)S(1)} custom-call(bf16[8,2,2,208,128]{4,3,2,1,0:T(8,128)(2,1)S(1)} %bitcast.16), custom_call_target="tpu_custom_call" | custom-call | flops 10000000 | bytes 60000000 | tf_op jit(solution)/shard_map/reduce_rows/pallas_call | solution.py:558
  135.9 0.6 slice_bitcast_fusion
  136.5 0.0 all-to-all-done.1
  136.5 2.0 %finish.1 = (bf16[768,512]{1,0:T(8,128)(2,1)}, f32[64,1024]{1,0:T(8,128)}, f32[64,512]{1,0:T(8,128)}, f32[64,128]{1,0:T(8,128)S(1)}) custom-call(s32[3,32]{1,0:T(4,128)S(1)} %get-tuple-element.28.lens_ref.meta_ref, bf16[32,48,512]{2,1,0:T(8,128)(2,1)S(1)} %bitcast.15, bf16[13,64,128]{2,1,0:T(8,128)(2,1)S(1)} %bitcast.18), custom_call_target="tpu_custom_call" | custom-call | tf_op jit(solution)/shard_map/finish/pallas_call | solution.py:726
  138.6 0.7 slice_reduce_fusion
  139.3 0.7 copy.19
  (6 shorter events, 0.0 us)
Async XLA Ops:
  0.6 1.1 copy-start
  1.8 0.7 copy-start.1
  2.4 0.7 copy-start.2
  9.2 6.5 %copy-start.10 = (f32[512,31]{0,1:T(8,128)S(1)}, f32[512,31]{0,1:T(8,128)}, u32[]{:S(2)}) copy-start(f32[512,31]{0,1:T(8,128)} %param.16) | copy-start | bytes 190468
  9.3 6.5 %copy-start.3 = (bf16[1536,512]{1,0:T(8,128)(2,1)S(1)}, bf16[1536,512]{1,0:T(8,128)(2,1)}, u32[]{:S(2)}) copy-start(bf16[1536,512]{1,0:T(8,128)(2,1)} %frames_ref.1) | copy-start | bytes 4718596
  9.3 6.5 %copy-start.8 = (f32[512]{0:T(512)S(1)}, f32[512]{0:T(512)}, u32[]{:S(2)}) copy-start(f32[512]{0:T(512)} %param.14) | copy-start | bytes 6148
  9.3 49.2 %all-to-all-start = ((bf16[8,4,48,512]{3,2,1,0:T(8,128)(2,1)}), bf16[8,4,48,512]{3,2,1,0:T(8,128)(2,1)S(1)}, u32[]{:S(2)}, u32[]{:S(2)}) async-start(bf16[8,4,48,512]{3,2,1,0:T(8,128)(2,1)} %bitcast.2), calls=%async_computation | async-start | bytes 3145728 | tf_op jit(solution)/shard_map/all_to_all | solution.py:613
  15.8 1.2 copy-start.4
  17.0 41.5 %copy-start.7 = (f32[512]{0:T(512)S(1)}, f32[512]{0:T(512)}, u32[]{:S(2)}) copy-start(f32[512]{0:T(512)} %param.18) | copy-start | bytes 6148
  17.0 41.5 %copy-start.9 = (f32[512]{0:T(512)S(1)}, f32[512]{0:T(512)}, u32[]{:S(2)}) copy-start(f32[512]{0:T(512)} %param.17) | copy-start | bytes 6148
  58.5 1.0 copy-start.6
  69.2 13.2 %copy-start.5 = (bf16[512,1024]{1,0:T(8,128)(2,1)S(1)}, bf16[512,1024]{1,0:T(8,128)(2,1)}, u32[]{:S(2)}) copy-start(bf16[512,1024]{1,0:T(8,128)(2,1)} %w_in_ref.3) | copy-start | bytes 3145732
  78.6 58.0 %all-to-all-start.1 = ((bf16[8,4,48,512]{3,2,1,0:T(8,128)(2,1)}), bf16[8,4,48,512]{3,2,1,0:T(8,128)(2,1)S(1)}, u32[]{:S(2)}, u32[]{:S(2)}) async-start(bf16[8,4,48,512]{3,2,1,0:T(8,128)(2,1)} %bitcast.6), calls=%async_computation.1 | async-start | bytes 3145728 | tf_op jit(solution)/shard_map/all_to_all | solution.py:613

commit v4 on v3

--- a/solution.py
+++ b/solution.py
@@ -267,7 +267,7 @@
                 ].astype(jnp.bfloat16)
 
 
-def plan_kernel(slots, lens_ref, owners_ref, up_ref, out_ref, meta_ref, stage, counts):
+def plan_kernel(slots, lens_ref, owners_ref, up_ref, out_ref, meta_ref, stage, counts, begin):
     me = lax.axis_index("bucket")
     own_rows, width = up_ref.shape
     span = out_ref.shape[1]
@@ -280,17 +280,24 @@
 
     def look(i, carry):
         found, start = carry
-        mine = owners_ref[0, i] == me
-
-        @pl.when(mine)
-        def _():
-            meta_ref[2, found] = start
-            for c in range(blocks):
-                out_ref[found, :, lane(c)] = stage[c, pl.ds(start, span)].astype(jnp.bfloat16)
-
-        return found + mine.astype(jnp.int32), start + jnp.where(mine, lens_ref[0, i], 0)
-
-    lax.fori_loop(0, loaders * slots, look, (jnp.int32(0), jnp.int32(0)))
+        for j in range(SUB):
+            at = i * SUB + j
+            mine = owners_ref[0, at] == me
+            begin[found] = start
+            found = found + jnp.where(mine, 1, 0)
+            start = start + jnp.where(mine, lens_ref[0, at], 0)
+        return found, start
+
+    lax.fori_loop(0, loaders * slots // SUB, look, (jnp.int32(0), jnp.int32(0)))
+
+    def move(i, carry):
+        start = begin[i]
+        meta_ref[2, i] = start
+        for c in range(blocks):
+            out_ref[i, :, lane(c)] = stage[c, pl.ds(start, span)].astype(jnp.bfloat16)
+        return carry
+
+    lax.fori_loop(0, slots, move, 0)
 
     def clear(i, carry):
         counts[i] = 0
@@ -603,10 +610,14 @@
         in_specs=[in_smem, in_smem, in_vmem],
         out_specs=[in_vmem, in_smem],
         out_shape=[slot_shape, jax.ShapeDtypeStruct((3, slot_count), jnp.int32)],
-        scratch_shapes=[stage_shape, pltpu.SMEM((loaders,), jnp.int32)],
+        scratch_shapes=[
+            stage_shape,
+            pltpu.SMEM((loaders,), jnp.int32),
+            pltpu.SMEM((slot_count + 1,), jnp.int32),
+        ],
         compiler_params=pltpu.CompilerParams(vmem_limit_bytes=VMEM_LIMIT),
         name="plan",
-    )(lengths, owners, upstream)
+    )(in_hbm(lengths), in_hbm(owners), in_hbm(upstream))
 
     def exchange(slots):
         slots = slots.reshape(loaders, pair_count, span, width)

time: 141 us -> 136 us (0.965)
  local copies, waits for them, and re-layouts: 6.74 us -> 4.26 us
  Pallas kernels: 122 us -> 120 us
    unnamed x23 -> x17, local copies, waits for them, and re-layouts: 5.45 us -> 2.97 us
    pallas_call x1, Pallas kernels: 6.11 us -> 3.96 us  [local(): pl.pallas_call(functools.partial(plan_kernel, slot_count), in_specs=[in_s...]
  transfers between devices with their start and end apart: 2 -> 2, of which waited for: 0 -> 0; matrix products, arithmetic and copies ran while one was open for 0% -> 0% of each run, Pallas kernels for 68% -> 70%
where the time goes in v4:
time: 136 us; the launch traced here: 135 us
  Pallas kernels  120 us (88%)
  starting transfers between devices  10.4 us (8%)
  local copies, waits for them, and re-layouts  4.26 us (3%)
    pallas_call x2, Pallas kernels, sum_everywhere(): pl.pallas_call(functools.partial(sum_kernel, groups, owners), out_shape=j...  35.7 us
    pallas_call x1, Pallas kernels, local(): pl.pallas_call(functools.partial(backward_kernel, group, span, taps, tota...  29.1 us
    pallas_call x1, Pallas kernels, reduce_rows(): pl.pallas_call(functools.partial(reduce_kernel, groups, owners), out_shap...  24.3 us
    pallas_call x1, Pallas kernels, local(): pl.pallas_call(functools.partial(forward_kernel, group, span, taps), grid...  15.1 us
    all_to_all x2, starting transfers between devices, exchange(): lax.all_to_all(slots, 'bucket', split_axis=0, concat_axis=0, tiled=True)  10.4 us
    pallas_call x1, Pallas kernels, local(): pl.pallas_call(functools.partial(middle_kernel, group, span, total_frames...  9.6 us
    pallas_call x1, Pallas kernels, local(): pl.pallas_call(functools.partial(plan_kernel, slot_count), in_specs=[in_s...  3.96 us
    unnamed x17, local copies, waits for them, and re-layouts  2.97 us
  transfers between devices with their start and end apart: 2, of which 0 were waited for; matrix products, arithmetic and copies ran while one was open for 0% of the time, Pallas kernels for 70%

profile of v4, /device:TPU:1, one launch (start us, length us, event | category | flops | bytes accessed | tf_op | source)
XLA Modules:
  0.0 135.3 jit_solution(869210817985733074)
XLA Ops:
  0.6 4.0 %plan.1 = (bf16[32,48,512]{2,1,0:T(8,128)(2,1)}, s32[3,32]{1,0:T(4,128)S(1)}) custom-call(s32[1,256]{1,0:T(1,128)} %lens_ref.1, s32[1,256]{1,0:T(1,128)} %owners_ref.1, bf16[768,512]{1,0:T(8,128)(2,1)} %up_ref.1), custom_call_target="tpu_custom_call" | custom-call | tf_op jit(solution)/shard_map/plan/pallas_call | solution.py:608
  4.6 0.0 copy-start.7
  4.6 0.0 copy-start
  4.6 0.0 copy-start.5
  4.6 6.5 %all-to-all-start = ((bf16[8,4,48,512]{3,2,1,0:T(8,128)(2,1)}), bf16[8,4,48,512]{3,2,1,0:T(8,128)(2,1)S(1)}, u32[]{:S(2)}, u32[]{:S(2)}) async-start(bf16[8,4,48,512]{3,2,1,0:T(8,128)(2,1)} %bitcast.2), calls=%async_computation | async-start | bytes 3145728 | tf_op jit(solution)/shard_map/all_to_all | solution.py:624
  11.1 0.0 copy-done.7
  11.2 0.0 copy-done
  11.2 0.0 copy-done.5
  11.2 0.0 copy-start.1
  11.2 1.2 copy-done.1
  12.4 0.0 copy-start.4
  12.4 0.0 copy-start.6
  12.4 15.1 %forward.1 = (f32[1536,512]{1,0:T(8,128)}, f32[8,128]{1,0:T(8,128)S(1)}, f32[1536,512]{1,0:T(8,128)}, f32[1536,128]{1,0:T(8,128)}, f32[1536,512]{1,0:T(8,128)}, /*index=5*/f32[1536,512]{1,0:T(8,128)}) custom-call(s32[3,32]{1,0:T(4,128)S(1)} %get-tuple-element.28.lens_ref.meta_ref, bf16[1536,512]{1,0:T(8,128)(2,1)S(1)} %copy-done, f32[1,512]{1,0:T(1,128)S(1)} %bitcast.21, ...), custom_call_target="tpu_custom_call" | custom-call | flops 2000000000 | bytes 40000000 | tf_op jit(solution)/shard_map/forward/pallas_call | solution.py:644
  27.5 26.4 %sum_everywhere_0.1.total_ref = f32[8,128]{1,0:T(8,128)S(1)} custom-call(f32[8,128]{1,0:T(8,128)S(1)} %get-tuple-element.31.part_ref), custom_call_target="tpu_custom_call" | custom-call | flops 1000000 | bytes 20000000 | tf_op jit(solution)/shard_map/sum_everywhere_0/pallas_call | solution.py:404
  53.9 0.0 all-to-all-done
  53.9 0.0 copy-done.4
  53.9 0.0 copy-done.6
  53.9 0.0 copy-start.3
  53.9 1.0 copy-done.3
  55.0 9.6 %middle.1 = (bf16[32,48,512]{2,1,0:T(8,128)(2,1)}, f32[1536,512]{1,0:T(8,128)}, f32[8,128]{1,0:T(8,128)S(1)}, f32[512,512]{1,0:T(8,128)}) custom-call(s32[3,32]{1,0:T(4,128)S(1)} %get-tuple-element.28.lens_ref.meta_ref, f32[1536,512]{1,0:T(8,128)} %get-tuple-element.29.conv_ref, bf16[32,48,512]{2,1,0:T(8,128)(2,1)S(1)} %bitcast.17, ...), custom_call_target="tpu_custom_call" | custom-call | flops 3000000000 | bytes 20000000 | tf_op jit(solution)/shard_map/middle/pallas_call | solution.py:671
  64.6 0.0 copy-start.2
  64.6 9.3 %sum_everywhere_1.1.back_ref = f32[8,128]{1,0:T(8,128)S(1)} custom-call(f32[8,128]{1,0:T(8,128)S(1)} %get-tuple-element.33.part_ref), custom_call_target="tpu_custom_call" | custom-call | flops 1000000 | bytes 20000000 | tf_op jit(solution)/shard_map/sum_everywhere_1/pallas_call | solution.py:404
  73.9 3.9 %all-to-all-start.1 = ((bf16[8,4,48,512]{3,2,1,0:T(8,128)(2,1)}), bf16[8,4,48,512]{3,2,1,0:T(8,128)(2,1)S(1)}, u32[]{:S(2)}, u32[]{:S(2)}) async-start(bf16[8,4,48,512]{3,2,1,0:T(8,128)(2,1)} %bitcast.6), calls=%async_computation.1 | async-start | bytes 3145728 | tf_op jit(solution)/shard_map/all_to_all | solution.py:624
  77.8 0.0 copy-done.2
  77.8 29.1 %backward.1 = (bf16[1536,512]{1,0:T(8,128)(2,1)}, bf16[8,832,128]{2,1,0:T(8,128)(2,1)S(1)}) custom-call(s32[3,32]{1,0:T(4,128)S(1)} %get-tuple-element.28.lens_ref.meta_ref, f32[1536,512]{1,0:T(8,128)} %get-tuple-element.35.normed_ref, f32[1536,128]{1,0:T(8,128)} %get-tuple-element.36.inverse_ref, f32[1536,512]{1,0:T(8,128)} %get-tuple-element.37.linear_ref, ...), custom_call_target="tpu_custom_call" | custom-call | flops 6000000000 | bytes 80000000 | tf_op jit(solution)/shard_map/backward/pallas_call | solution.py:701
  106.9 24.3 %reduce_rows.1 = bf16[4,208,128]{2,1,0:T(8,128)(2,1)S(1)} custom-call(bf16[8,2,2,208,128]{4,3,2,1,0:T(8,128)(2,1)S(1)} %bitcast.16), custom_call_target="tpu_custom_call" | custom-call | flops 10000000 | bytes 60000000 | tf_op jit(solution)/shard_map/reduce_rows/pallas_call | solution.py:565
  131.3 0.6 slice_bitcast_fusion
  131.8 0.0 all-to-all-done.1
  131.8 2.0 %finish.1 = (bf16[768,512]{1,0:T(8,128)(2,1)}, f32[64,1024]{1,0:T(8,128)}, f32[64,512]{1,0:T(8,128)}, f32[64,128]{1,0:T(8,128)S(1)}) custom-call(s32[3,32]{1,0:T(4,128)S(1)} %get-tuple-element.28.lens_ref.meta_ref, bf16[32,48,512]{2,1,0:T(8,128)(2,1)S(1)} %bitcast.15, bf16[13,64,128]{2,1,0:T(8,128)(2,1)S(1)} %bitcast.18), custom_call_target="tpu_custom_call" | custom-call | tf_op jit(solution)/shard_map/finish/pallas_call | solution.py:737
  133.9 0.7 slice_reduce_fusion
  134.6 0.7 copy.19
  (1 shorter events, 0.0 us)
Async XLA Ops:
  4.6 6.5 %copy-start.7 = (f32[512,31]{0,1:T(8,128)S(1)}, f32[512,31]{0,1:T(8,128)}, u32[]{:S(2)}) copy-start(f32[512,31]{0,1:T(8,128)} %param.16) | copy-start | bytes 190468
  4.6 6.5 %copy-start = (bf16[1536,512]{1,0:T(8,128)(2,1)S(1)}, bf16[1536,512]{1,0:T(8,128)(2,1)}, u32[]{:S(2)}) copy-start(bf16[1536,512]{1,0:T(8,128)(2,1)} %frames_ref.1) | copy-start | bytes 4718596
  4.6 6.5 %copy-start.5 = (f32[512]{0:T(512)S(1)}, f32[512]{0:T(512)}, u32[]{:S(2)}) copy-start(f32[512]{0:T(512)} %param.14) | copy-start | bytes 6148
  4.6 49.2 %all-to-all-start = ((bf16[8,4,48,512]{3,2,1,0:T(8,128)(2,1)}), bf16[8,4,48,512]{3,2,1,0:T(8,128)(2,1)S(1)}, u32[]{:S(2)}, u32[]{:S(2)}) async-start(bf16[8,4,48,512]{3,2,1,0:T(8,128)(2,1)} %bitcast.2), calls=%async_computation | async-start | bytes 3145728 | tf_op jit(solution)/shard_map/all_to_all | solution.py:624
  11.2 1.2 copy-start.1
  12.4 41.5 %copy-start.4 = (f32[512]{0:T(512)S(1)}, f32[512]{0:T(512)}, u32[]{:S(2)}) copy-start(f32[512]{0:T(512)} %param.18) | copy-start | bytes 6148
  12.4 41.5 %copy-start.6 = (f32[512]{0:T(512)S(1)}, f32[512]{0:T(512)}, u32[]{:S(2)}) copy-start(f32[512]{0:T(512)} %param.17) | copy-start | bytes 6148
  53.9 1.0 copy-start.3
  64.6 13.2 %copy-start.2 = (bf16[512,1024]{1,0:T(8,128)(2,1)S(1)}, bf16[512,1024]{1,0:T(8,128)(2,1)}, u32[]{:S(2)}) copy-start(bf16[512,1024]{1,0:T(8,128)(2,1)} %w_in_ref.3) | copy-start | bytes 3145732
  73.9 58.0 %all-to-all-start.1 = ((bf16[8,4,48,512]{3,2,1,0:T(8,128)(2,1)}), bf16[8,4,48,512]{3,2,1,0:T(8,128)(2,1)S(1)}, u32[]{:S(2)}, u32[]{:S(2)}) async-start(bf16[8,4,48,512]{3,2,1,0:T(8,128)(2,1)} %bitcast.6), calls=%async_computation.1 | async-start | bytes 3145728 | tf_op jit(solution)/shard_map/all_to_all | solution.py:624
